TPU v7x, 32 devices: a whole 2x2x4 slice. The times are simulated.
32 devices in a mesh: pts: 8 (over z, y), grp: 4 (over x, core).
Axes of the slice: x: 2, y: 2, z: 4, core: 2. Of those that a mesh axis runs over, the one named last changes fastest.
Arguments:
- jacobian: bfloat16 [32, 6, 128, 3, 256], P(('pts', 'grp')), may hold values from -0.21875 to 0.21875
- point_blocks: float32 [32, 6, 256], P(('pts', 'grp')), may hold values from -0.5 to 4, as said below
- point_grad: bfloat16 [32, 3, 256], P(('pts', 'grp')), may hold values from -6 to 6
- camera_grad: float32 [32, 128], P(('pts', 'grp')), may hold values from -6 to 6
- damping: float32 [32, 128], replicated, may hold values from 1 to 8
- incidence: int32 [32, 6], P(('pts', 'grp')), may hold values from 0 to 31, as said below
- tile_owner: int32 [8], replicated, may hold values from 0 to 7, each once
- front_first: int32 [1], replicated, may hold values from 0 to 31
Outputs:
- tiles_out: float32 [256, 128, 128], P(('pts', 'grp'))
- rhs_out: float32 [32, 128], P(('pts', 'grp'))
- front_panel: float32 [2304, 512], P(None, 'grp')
Inputs may be any that keep to these rules, and one draw needn't show every extreme that they name: `incidence`: point cluster p names 6 different camera clusters, all among (p + t) mod 32 for t from 0 to 7. `point_blocks`: each point's diagonal entries exceed the sum of the magnitudes of the two off-diagonal entries of their row by 0.1 or more. `tile_owner`: A permutation of the pts indices.
All inputs are finite; a program needn't handle non-finite values.
Results may differ from a plain program's by a relative error of at most 0.0022.
Values sent between devices are 32-bit elements; how exact they have to be, the bound alone decides.
No kernel may reach another device: no remote copies, remote signals or barrier semaphores. Data moves between devices by JAX's collectives and lax.ppermute only.
A program may use at most 128 MiB of HBM per device.

v0:
```python
import functools

import jax
import jax.numpy as jnp
from jax import lax
from jax.experimental import pallas as pl
from jax.experimental.pallas import tpu as pltpu
from jax.sharding import PartitionSpec as P


TOUCH = 6
BAND = 8
FRONT = 4
BEFORE = BAND - 1
WINDOW = 2 * BAND - 2 + FRONT
PAIRS = TOUCH * (TOUCH + 1) // 2
GROUP = 8
SPAN = 2 * BAND - 1
STRIP = 8
AXES = ("pts", "grp")
VM = pltpu.VMEM
SM = pltpu.SMEM


def spec(space):
    return pl.BlockSpec(memory_space=space)


def size_of(shape, dtype):
    total = jnp.dtype(dtype).itemsize
    for extent in shape:
        total *= extent
    return total


def call(kernel, out_shapes, args, spaces, scratch=(), flops=0):
    moved = sum(size_of(x.shape, x.dtype) for x, s in zip(args, spaces) if s is VM)
    moved += sum(size_of(x.shape, x.dtype) for x in jax.tree.leaves(out_shapes))
    kept = 0
    for x in scratch:
        if x.memory_space is VM:
            kept += size_of(x.shape, x.dtype)
    limit = min(moved + kept + (8 << 20), 60 << 20)
    return pl.pallas_call(
        kernel,
        out_shape=out_shapes,
        in_specs=[spec(s) for s in spaces],
        out_specs=[spec(VM)] * len(out_shapes),
        scratch_shapes=list(scratch),
        cost_estimate=pl.CostEstimate(flops=flops, bytes_accessed=moved, transcendentals=0),
        compiler_params=pltpu.CompilerParams(vmem_limit_bytes=limit),
    )(*args)


NT = (((1,), (1,)), ((), ()))
TN = (((0,), (0,)), ((), ()))
NN = (((1,), (0,)), ((), ()))


def product(a, b, dims):
    return lax.dot_general(a, b, dims, preferred_element_type=jnp.float32)


def halves(x):
    high = x.astype(jnp.bfloat16)
    return high, (x - high.astype(jnp.float32)).astype(jnp.bfloat16)


def product3(a, b, dims):
    return (
        product(a[0], b[0], dims) + product(a[0], b[1], dims) + product(a[1], b[0], dims)
    )


def pair_index(a, b):
    return (TOUCH - 1) * a - (a * (a - 1)) // 2 + b


def pair_kernel(dims, meta, incidence, jac, blocks, grad, cam, *refs):
    rows, points, piece, grp_count, clusters = dims
    outs, (out, scaled, plain, rhs, pulls) = refs[:GROUP], refs[GROUP:]
    slots = [lax.rem(incidence[0, k] + clusters - meta[2], clusters) for k in range(TOUCH)]
    ranks = [
        sum((slots[m] < slots[k]).astype(jnp.int32) for m in range(TOUCH) if m != k)
        for k in range(TOUCH)
    ]
    v00, v11, v22 = blocks[0:1, :], blocks[1:2, :], blocks[2:3, :]
    v01, v02, v12 = blocks[3:4, :], blocks[4:5, :], blocks[5:6, :]
    a00 = v11 * v22 - v12 * v12
    a11 = v00 * v22 - v02 * v02
    a22 = v00 * v11 - v01 * v01
    a01 = v02 * v12 - v01 * v22
    a02 = v01 * v12 - v11 * v02
    a12 = v01 * v02 - v00 * v12
    inv = 1.0 / (v00 * a00 + v01 * a01 + v02 * a02)
    vinv = [
        [a00 * inv, a01 * inv, a02 * inv],
        [a01 * inv, a11 * inv, a12 * inv],
        [a02 * inv, a12 * inv, a22 * inv],
    ]
    rhs[...] = jnp.zeros_like(rhs)
    rhs[0:1, :] = cam[...]
    wide_grad = grad[...].astype(jnp.float32)
    for c in range(3):
        pulls[:, c * points : (c + 1) * points] = jnp.broadcast_to(
            wide_grad[c : c + 1, :], (16, points)
        ).astype(jnp.bfloat16)
    for a in range(TOUCH):
        k = sum(jnp.where(ranks[m] == a, m, 0) for m in range(TOUCH))
        t = sum(jnp.where(ranks[m] == a, slots[m], 0) for m in range(TOUCH))
        parts = [jac[c, k] for c in range(3)]
        wide = [x.astype(jnp.float32) for x in parts]
        for c in range(3):
            total = wide[0] * vinv[0][c] + wide[1] * vinv[1][c] + wide[2] * vinv[2][c]
            scaled[a, :, c * points : (c + 1) * points] = total.astype(jnp.bfloat16)
            plain[a * rows : (a + 1) * rows, c * points : (c + 1) * points] = parts[c]
        pulled = product(pulls[...], scaled[a], NT)
        rhs[pl.ds(t, 1), :] = rhs[pl.ds(t, 1), :] - pulled[0:1, :]
    for a in range(TOUCH):
        tiles = product(scaled[a], plain[a * rows : TOUCH * rows, :], NT)
        for b in range(a, TOUCH):
            at = pair_index(a, b) * piece
            for e in range(GROUP):
                first = (e % grp_count) * (rows // grp_count) + (e // grp_count) * piece
                out[e, at : at + piece, :] = tiles[
                    first : first + piece, (b - a) * rows : (b - a + 1) * rows
                ]
    lane = lax.broadcasted_iota(jnp.int32, (BAND, rows), 1)
    early = lax.rem(lane // BAND, BAND)
    late = early + lax.rem(lane, BAND)
    ones = jnp.ones_like(lane)
    none = jnp.zeros_like(lane)
    less, less_late, hit, hit_late = none, none, none, none
    for k in range(TOUCH):
        less = less + jnp.where(early > slots[k], ones, none)
        less_late = less_late + jnp.where(late > slots[k], ones, none)
        hit = hit + jnp.where(early == slots[k], ones, none)
        hit_late = hit_late + jnp.where(late == slots[k], ones, none)
    pick = jnp.where(hit * hit_late > 0, pair_index(less, less_late), -1).astype(jnp.float32)
    tail = PAIRS * piece
    for e in range(GROUP):
        out[e, tail : tail + BAND, :] = rhs[...]
        out[e, tail + BAND : tail + 2 * BAND, :] = pick
    place = lax.rem(meta[2], GROUP)
    for bit in range(GROUP):
        outs[bit][...] = out[place ^ bit]


def merge_kernel(dims, owner, meta, *refs):
    piece, pts_count, capacity, sends = dims
    arrived, outs = refs[:GROUP], refs[GROUP : GROUP + sends]
    got, out, rhs, table, pick, sem = refs[GROUP + sends :]
    place = lax.rem(meta[2], GROUP)
    for bit in range(GROUP):
        got[place ^ bit] = arrived[bit][...]
    flip = meta[0] if sends > 1 else 0
    base = lax.rem(meta[2] // GROUP * (GROUP * BAND), pts_count)
    tail = PAIRS * piece
    for j in range(GROUP):
        row = got[j, tail + BAND : tail + 2 * BAND, :]
        table[j : j + 1, :] = row[0:1, :].astype(jnp.int32)
    copy = pltpu.make_async_copy(table, pick, sem)
    copy.start()
    copy.wait()
    for row in range(SPAN):
        for offset in range(BAND):
            if row + offset >= SPAN:
                continue
            total = None
            for j in range(GROUP):
                t = row - j
                if t < 0 or t + offset > BAND - 1:
                    continue
                at = pick[j, t * BAND + offset]
                start = pl.multiple_of(jnp.maximum(at, 0) * piece, piece)
                value = jnp.where(at >= 0, got[j, pl.ds(start, piece), :], 0.0)
                total = value if total is None else total + value
            relative = BAND * row + offset
            dest = owner[lax.rem(base + relative, pts_count)]
            slot = relative // pts_count
            out[dest ^ flip, slot * piece : (slot + 1) * piece, :] = total
    rhs[...] = jnp.zeros_like(rhs)
    for j in range(GROUP):
        rhs[j : j + BAND, :] = rhs[j : j + BAND, :] + got[j, PAIRS * piece : PAIRS * piece + BAND, :]
    for dest in range(pts_count):
        out[dest, capacity * piece : capacity * piece + 2 * BAND, :] = rhs[...]
    for bit in range(sends):
        outs[bit][...] = out[bit] if sends > 1 else out[...]


def residue_of(owner, meta, pts_count):
    return sum(jnp.where(owner[i] == meta[0], i, 0) for i in range(pts_count))


def owner_kernel(
    dims, owner, meta, front, damping, *refs
):
    piece, pts_count, capacity, grp_count, quarter, clusters, sets, sends = dims
    arrived = refs[:sends]
    outs = refs[sends : sends + grp_count]
    direct, mirror, reduced, got, rows_out = refs[sends + grp_count :]
    for bit in range(sends):
        if sends > 1:
            got[meta[0] ^ bit] = arrived[bit][...]
        else:
            got[...] = arrived[0][...]
    residue, my_grp, start = residue_of(owner, meta, pts_count), meta[1], front[0]
    members = GROUP // grp_count
    planes = clusters // GROUP
    cols = rows_out.shape[3]
    offset = lax.rem(residue, BAND)
    part = residue // BAND
    stride = pts_count // BAND
    diag = (
        lax.broadcasted_iota(jnp.int32, (quarter, cols), 0) + my_grp * quarter
        == lax.broadcasted_iota(jnp.int32, (quarter, cols), 1)
    )
    diag = diag & (offset == 0)
    for m in range(BAND * grp_count):
        home = (residue + pts_count * m) // BAND
        plane = home // GROUP
        row = lax.rem(home, GROUP)
        before = lax.rem(plane + planes - 1, planes)
        near = (BAND * row + offset) // pts_count
        far = (BAND * (row + GROUP) + offset) // pts_count
        has_far = row + GROUP + offset < SPAN
        far = jnp.where(has_far, far, 0)
        for y in range(members):
            value = got[plane * members + y, pl.ds(pl.multiple_of(near * piece, piece), piece), :]
            extra = got[before * members + y, pl.ds(pl.multiple_of(far * piece, piece), piece), :]
            total = value + jnp.where(has_far, extra, 0.0)
            part_diag = diag[y * piece : (y + 1) * piece, :]
            total = total + jnp.where(part_diag, damping[pl.ds(home, 1), :], 0.0)
            rows_out[(m // BAND) ^ my_grp, m % BAND, y * piece : (y + 1) * piece, :] = total
    for i in range(sets):
        j = lax.rem(part + 2 * clusters - start, stride) + stride * i
        home = lax.rem(start + jnp.minimum(j, FRONT - 1), clusters)
        at = (BAND * home + offset) // pts_count
        value = rows_out[(at // BAND) ^ my_grp, lax.rem(at, BAND)]
        j = lax.rem(part + 2 * clusters - start + offset, stride) + stride * i
        home = lax.rem(start + jnp.minimum(j, FRONT - 1) + clusters - offset, clusters)
        at = (BAND * home + offset) // pts_count
        other = rows_out[(at // BAND) ^ my_grp, lax.rem(at, BAND)]
        for layer in range(direct.shape[0] // (sets * quarter)):
            at = (layer * sets + i) * quarter
            direct[at : at + quarter, :] = value
            mirror[at : at + quarter, :] = other
    for bit in range(grp_count):
        for i in range(BAND):
            outs[bit][i * quarter : (i + 1) * quarter, :] = rows_out[bit, i]
    tail = capacity * piece
    for plane in range(planes):
        before = (plane + planes - 1) % planes
        reduced[plane * GROUP : (plane + 1) * GROUP, :] = (
            got[plane * members, tail : tail + BAND, :]
            + got[before * members, tail + BAND : tail + 2 * BAND, :]
        )


def gather(gathered, sides, meta, clusters, ring):
    layers = clusters // GROUP
    place, level = lax.rem(meta[2], GROUP), meta[2] // GROUP
    for i in range(GROUP // 2):
        for z in range(layers):
            at = lax.rem(level + layers - z, layers) if ring else z
            at = at * GROUP + (place ^ (2 * i))
            count = gathered.shape[1]
            ref, first = sides[i]
            gathered[at] = ref[first + z * count : first + (z + 1) * count, :]
            ref, first = sides[GROUP // 2 + i]
            gathered[at ^ 1] = ref[first + z * count : first + (z + 1) * count, :]


def fetch(gathered, owner, tile, slot, dims):
    pts_count, grp_count, quarter = dims
    source = owner[lax.rem(tile, pts_count)] * grp_count
    rows = slice(slot * quarter, (slot + 1) * quarter)
    return jnp.concatenate([gathered[source + g, rows, :] for g in range(grp_count)], axis=0)


def factor_kernel(dims, meta, front, owner, reduced, *refs):
    pts_count, grp_count, quarter, clusters, ring = dims
    sides = [(ref, 0) for ref in refs[:GROUP]]
    tail_out, solve_high, solve_low, behind_high, behind_low = refs[GROUP : GROUP + 5]
    upper, behind, gathered, work, done, square, wide = refs[GROUP + 5 :]
    rows = done.shape[0]
    width = FRONT * rows
    start = front[0]
    stride = pts_count // BAND
    after = BAND - 1
    last = after * rows
    gather(gathered, sides, meta, clusters, ring)
    work[rows:, :] = jnp.zeros((STRIP, 2 * rows), jnp.float32)
    wide[...] = jnp.zeros_like(wide)
    upper[...] = jnp.zeros_like(upper)
    square[...] = jnp.zeros_like(square)
    row_id = lax.broadcasted_iota(jnp.int32, (rows, 1), 0)
    col_id = lax.broadcasted_iota(jnp.int32, (1, rows), 1)
    eye = (row_id == col_id).astype(jnp.float32)
    for j in range(FRONT):
        home = lax.rem(start + j, clusters)
        for e in range(BAND):
            tile = fetch(
                gathered, owner, BAND * home + e, j // stride, (pts_count, grp_count, quarter)
            )
            if j + e < FRONT:
                if e == 0:
                    tile = 0.5 * (tile + tile.T)
                square[j, :, (j + e) * rows : (j + e + 1) * rows] = tile
            else:
                at = (j + e - FRONT) * rows
                wide[at : at + rows, j * rows : (j + 1) * rows] = tile.T
        wide[last : last + 1, j * rows : (j + 1) * rows] = reduced[pl.ds(home, 1), :]
    for j in range(FRONT):
        here = j * rows
        work[0:rows, 0:rows] = square[j, :, here : here + rows]
        work[0:rows, rows : 2 * rows] = eye
        eliminate(work, done, rows)
        inverse = jnp.where(row_id >= col_id, done[:, rows : 2 * rows], 0.0)
        pair = halves(inverse)
        upper[j, :, here : here + rows] = jnp.where(row_id <= col_id, done[:, 0:rows], 0.0)
        parts = []
        if j < FRONT - 1:
            parts.append(square[j, :, here + rows : width])
        if j > 0:
            parts.append(square[j, :, width : width + here])
        line = product3(pair, halves(jnp.concatenate(parts, axis=1)), NN)
        ahead = width - here - rows
        if ahead:
            upper[j, :, here + rows :] = line[:, 0:ahead]
        solve = jnp.concatenate([line[:, ahead:], inverse], axis=1) if j else inverse
        high, low = halves(solve)
        solve_high[here : here + rows, 0 : here + rows] = high
        solve_low[here : here + rows, 0 : here + rows] = low
        if j < FRONT - 1:
            zero = jnp.zeros((rows, ahead), jnp.bfloat16)
            solve_high[here : here + rows, here + rows :] = zero
            solve_low[here : here + rows, here + rows :] = zero
            both = halves(line[:, 0:ahead])
            for i in range(j + 1, FRONT):
                skip = (i - j - 1) * rows
                left = tuple(x[:, skip : skip + rows] for x in both)
                right = tuple(
                    jnp.concatenate([x[:, skip:], y], axis=1) for x, y in zip(both, (high, low))
                )
                change = product3(left, right, TN)
                cut = width - i * rows
                square[i, :, i * rows : width] = square[i, :, i * rows : width] - change[:, 0:cut]
                square[i, :, width : width + here + rows] = (
                    square[i, :, width : width + here + rows] - change[:, cut:]
                )
    result = solve_rows(wide, solve_high, solve_low)
    high, low = halves(result)
    behind_high[...] = high
    behind_low[...] = low
    behind[...] = result
    first = pl.ds(pl.multiple_of(meta[1] * rows, rows), rows)
    for j in range(FRONT):
        tail_out[j * rows : (j + 1) * rows, :] = upper[meta[1], :, j * rows : (j + 1) * rows].T
    tail_out[FRONT * rows : FRONT * rows + last, :] = behind[0:last, first]
    for j in range(FRONT):
        at = FRONT * rows + last + 8 * j
        tail_out[at : at + 8, :] = result[last : last + 8, j * rows : (j + 1) * rows]


def eliminate(work, done, rows):
    lanes = lax.broadcasted_iota(jnp.int32, (STRIP, rows), 1)
    subs = lax.broadcasted_iota(jnp.int32, (STRIP, rows), 0)

    def strip(p, carry):
        now, past = carry
        at = pl.multiple_of(p * STRIP, STRIP)
        lhs = jnp.where(lanes >= at + STRIP, past[:, 0:rows], 0.0)
        work[0:rows, :] = work[0:rows, :] - product3(halves(lhs), halves(past), TN)
        ahead = work[pl.ds(at + STRIP, STRIP), :]
        now_a, now_i = now[:, 0:rows], now[:, rows : 2 * rows]
        next_a, next_i = ahead[:, 0:rows], ahead[:, rows : 2 * rows]
        shift = lax.rem(rows - at, rows)
        turned = pltpu.roll(now_a, shift, 1)
        turned_next = pltpu.roll(next_a, shift, 1)
        column = [jnp.broadcast_to(turned[:, i : i + 1], (STRIP, rows)) for i in range(STRIP)]
        below = [jnp.broadcast_to(turned_next[:, i : i + 1], (STRIP, rows)) for i in range(STRIP)]
        norm = jnp.zeros((STRIP, rows), jnp.float32)

        def row(value, i):
            return jnp.broadcast_to(value[i : i + 1, :], (STRIP, rows))

        for i in range(0, STRIP, 2):
            a, b, c = row(column[i], i), row(column[i + 1], i), row(column[i + 1], i + 1)
            det = a * c - b * b
            inv = 1.0 / a
            inv_second = a * (1.0 / det)
            ratio = b * inv
            norm = jnp.where(subs == i, lax.rsqrt(a), norm)
            norm = jnp.where(subs == i + 1, lax.rsqrt(det * inv), norm)
            scale = jnp.where(subs > i, column[i] * inv, 0.0)
            scale_next = below[i] * inv
            second = jnp.where(subs > i + 1, (column[i + 1] - scale * b) * inv_second, 0.0)
            second_next = (below[i + 1] - scale_next * b) * inv_second
            for k in range(i + 2, STRIP):
                top = row(column[k], i)
                low = row(column[k], i + 1) - ratio * top
                column[k] = column[k] - scale * top - second * low
                below[k] = below[k] - scale_next * top - second_next * low
            line_a, line_i = row(now_a, i), row(now_i, i)
            low_a = row(now_a, i + 1) - ratio * line_a
            low_i = row(now_i, i + 1) - ratio * line_i
            now_a = now_a - scale * line_a - second * low_a
            now_i = now_i - scale * line_i - second * low_i
            next_a = next_a - scale_next * line_a - second_next * low_a
            next_i = next_i - scale_next * line_i - second_next * low_i
        finished = jnp.concatenate([now_a * norm, now_i * norm], axis=1)
        done[pl.ds(at, STRIP), :] = finished
        return (jnp.concatenate([next_a, next_i], axis=1), finished)

    first = work[0:STRIP, :]
    lax.fori_loop(0, rows // STRIP, strip, (first, jnp.zeros_like(first)))


def solve_rows(wide, solve_high, solve_low):
    half = solve_high.shape[0] // 2
    high, low = halves(wide[...])
    left = product3(
        (high[:, :half], low[:, :half]),
        (solve_high[:half, :half], solve_low[:half, :half]),
        NT,
    )
    right = product3((high, low), (solve_high[half:, :], solve_low[half:, :]), NT)
    return jnp.concatenate([left, right], axis=1)


def update_kernel(dims, meta, front, owner, reduced, *refs):
    pts_count, grp_count, quarter, clusters, ring = dims
    first, swapped, second, third, fourth, kept_chunk = refs[:6]
    refs = refs[6:]
    count = first.shape[0]
    chunk = BAND * quarter
    crossed = (second, third, fourth)
    sides = [(first, 0)] + [(ref, 0) for ref in crossed]
    sides += [(swapped, 0)] + [(ref, count) for ref in crossed]
    chunks = (
        (kept_chunk, 0), (swapped, count), (second, 2 * count), (second, 2 * count + chunk)
    )
    tail, solve_high, solve_low, behind_high, behind_low = refs[:5]
    tiles_out, rhs_out, panel_out, wide, ahead_high, ahead_low, gathered = refs[5:]
    rows = tiles_out.shape[1]
    residue, my_grp, start = residue_of(owner, meta, pts_count), meta[1], front[0]
    device = meta[2]
    stride = pts_count // BAND
    gather(gathered, sides, meta, clusters, ring)
    wide[...] = jnp.zeros_like(wide)
    for j in range(FRONT):
        for i in range(j, BEFORE):
            e = BEFORE + j - i
            home = lax.rem(start + j + clusters - e, clusters)
            tile = fetch(
                gathered, owner, BAND * home + e, j // stride, (pts_count, grp_count, quarter)
            )
            wide[i * rows : (i + 1) * rows, j * rows : (j + 1) * rows] = tile
    result = solve_rows(wide, solve_high, solve_low)
    wide[...] = result
    high, low = halves(result)
    ahead_high[...] = high
    ahead_low[...] = low
    first = pl.ds(pl.multiple_of(my_grp * rows, rows), rows)
    panel_out[0 : BEFORE * rows, :] = wide[:, first]
    panel_out[BEFORE * rows :, :] = tail[0 : (BEFORE + FRONT) * rows, :]
    base = start + clusters - BEFORE

    def ahead(position):
        at = pl.ds(pl.multiple_of(position * rows, rows), rows)
        return (ahead_high[at, :], ahead_low[at, :])

    def past(position):
        at = pl.ds(pl.multiple_of((position - BEFORE - FRONT) * rows, rows), rows)
        return (behind_high[at, :], behind_low[at, :])

    def is_ahead(position):
        return position < BEFORE

    def is_past(position):
        return (position < WINDOW) & (position >= BEFORE + FRONT)

    for i in range(BAND):
        tile = residue + pts_count * (BAND * my_grp + i)
        home = tile // BAND
        offset = lax.rem(tile, BAND)
        one = lax.rem(home + 2 * clusters - base, clusters)
        two = lax.rem(home + offset + 2 * clusters - base, clusters)
        for bit in range(grp_count):
            at = pl.multiple_of((my_grp ^ bit) * quarter, quarter)
            ref, begin = chunks[bit]
            begin = begin + i * quarter
            tiles_out[i, pl.ds(at, quarter), :] = ref[begin : begin + quarter, :]
        for left, right, test_left, test_right in (
            (ahead, ahead, is_ahead, is_ahead),
            (ahead, past, is_ahead, is_past),
            (past, past, is_past, is_past),
        ):
            @pl.when(test_left(one) & test_right(two))
            def _():
                tiles_out[i] = tiles_out[i] - product3(left(one), right(two), NT)

    position = lax.rem(device + 2 * clusters - base, clusters)
    mine = reduced[pl.ds(device, 1), :]
    rhs_out[...] = mine
    last = (BEFORE + FRONT) * rows
    front_row = [tail[last + 8 * j : last + 8 * j + 8, :] for j in range(FRONT)]
    for take, test in ((ahead, is_ahead), (past, is_past)):
        @pl.when(test(position))
        def _():
            known = halves(jnp.concatenate(front_row, axis=1))
            rhs_out[...] = mine - product3(known, take(position), NT)[0:1, :]

    @pl.when((position >= BEFORE) & (position < BEFORE + FRONT))
    def _():
        at = pl.multiple_of(last + 8 * (position - BEFORE), 8)
        rhs_out[...] = tail[pl.ds(at, 8), :][0:1, :]


def per_device(
    jacobian, point_blocks, point_grad, camera_grad, damping, incidence, tile_owner, front_first
):
    pts_count = lax.axis_size("pts")
    grp_count = lax.axis_size("grp")
    clusters = pts_count * grp_count
    my_grp = lax.axis_index("grp")
    my_pts = lax.axis_index("pts")
    device = my_pts * grp_count + my_grp
    rows = jacobian.shape[2]
    points = jacobian.shape[4]
    piece = rows // GROUP
    quarter = rows // grp_count
    capacity = (BAND * (SPAN - 1)) // pts_count + 1
    stride = pts_count // BAND
    sets = -(-FRONT // stride)
    f32 = jnp.float32
    layers = clusters // GROUP
    columns = [[GROUP * z + e for z in range(layers)] for e in range(GROUP)]
    swap = [(i, i ^ 1) for i in range(clusters)]

    def flip(values, axis, count):
        moved = [
            lax.ppermute(value, axis, [(p, p ^ (bit + 1)) for p in range(count)])
            for bit, value in enumerate(values[1:])
        ]
        return [values[0], *moved]

    def exchange(value, lists):
        return lax.all_to_all(
            value, AXES, split_axis=0, concat_axis=0, tiled=True, axis_index_groups=lists
        )

    lane = jnp.arange(8)
    meta = jnp.where(lane == 0, my_pts, jnp.where(lane == 1, my_grp, device)).astype(jnp.int32)
    bf16 = jnp.bfloat16
    jac = jnp.transpose(jacobian[0], (2, 0, 1, 3))
    block_rows = PAIRS * piece + 2 * BAND
    sent = call(
        functools.partial(pair_kernel, (rows, points, piece, grp_count, clusters)),
        [jax.ShapeDtypeStruct((block_rows, rows), f32)] * GROUP,
        (meta, incidence, jac, point_blocks[0], point_grad[0], camera_grad),
        (SM, SM, VM, VM, VM, VM),
        (
            pltpu.VMEM((GROUP, block_rows, rows), f32),
            pltpu.VMEM((TOUCH, rows, 3 * points), bf16),
            pltpu.VMEM((TOUCH * rows, 3 * points), bf16),
            pltpu.VMEM((BAND, rows), f32),
            pltpu.VMEM((16, 3 * points), bf16),
        ),
        flops=2 * PAIRS * rows * rows * 3 * points,
    )
    got = flip(sent, AXES, clusters)
    sends = pts_count if pts_count <= GROUP else 1
    send_rows = capacity * piece + 2 * BAND
    shape = (send_rows, rows) if sends > 1 else (pts_count, send_rows, rows)
    sent = call(
        functools.partial(merge_kernel, (piece, pts_count, capacity, sends)),
        [jax.ShapeDtypeStruct(shape, f32)] * sends,
        (tile_owner, meta, *got),
        (SM, SM) + (VM,) * GROUP,
        (
            pltpu.VMEM((GROUP, block_rows, rows), f32),
            pltpu.VMEM((pts_count, send_rows, rows), f32),
            pltpu.VMEM((2 * BAND, rows), f32),
            pltpu.VMEM((GROUP, rows), jnp.int32),
            pltpu.SMEM((GROUP, rows), jnp.int32),
            pltpu.SemaphoreType.DMA(()),
        ),
    )
    if sends > 1:
        got = flip(sent, "pts", pts_count)
    else:
        got = [lax.all_to_all(sent[0], "pts", split_axis=0, concat_axis=0, tiled=True)]
    copies = layers if layers > 4 else 1
    *chunks, direct, mirror, reduced = call(
        functools.partial(
            owner_kernel,
            (piece, pts_count, capacity, grp_count, quarter, clusters, sets, sends),
        ),
        [jax.ShapeDtypeStruct((BAND * quarter, rows), f32)] * grp_count
        + [
            jax.ShapeDtypeStruct((copies * sets * quarter, rows), f32),
            jax.ShapeDtypeStruct((copies * sets * quarter, rows), f32),
            jax.ShapeDtypeStruct((clusters, rows), f32),
        ],
        (tile_owner, meta, front_first, damping, *got),
        (SM, SM, SM, VM) + (VM,) * sends,
        (
            pltpu.VMEM((pts_count, send_rows, rows), f32),
            pltpu.VMEM((grp_count, BAND, quarter, rows), f32),
        ),
    )
    ring = layers <= 4

    def along(value):
        if not ring:
            return exchange(value, columns)
        moved = []
        for z in range(1, layers):
            pairs = [(p, (p + GROUP * z) % clusters) for p in range(clusters)]
            moved.append(lax.ppermute(value, AXES, pairs))
        return jnp.concatenate([value, *moved])

    def across(values):
        moved = []
        for i, value in enumerate(values):
            pairs = [(p, p ^ (2 * i + 2)) for p in range(clusters)]
            moved.append(lax.ppermute(value, AXES, pairs))
        return moved

    direct = along(direct)
    direct, mirror, *chunks = lax.optimization_barrier((direct, mirror, *chunks))
    mine = [direct, *across([direct] * 3)]
    theirs = [lax.ppermute(direct, AXES, swap)]
    mirror = along(mirror)
    swapped = lax.ppermute(jnp.concatenate([mirror, chunks[1], chunks[3]]), AXES, swap)
    count = mirror.shape[0]
    chunk = BAND * quarter
    both = jnp.concatenate([mirror, swapped[:count]])
    more = jnp.concatenate([both, chunks[2], swapped[count + chunk :]])
    both, more, *mine = lax.optimization_barrier((both, more, *mine))
    theirs += [lax.ppermute(x, AXES, swap) for x in mine[1:]]
    sides = [mirror, swapped, *across([more, both, both]), chunks[0]]

    width = FRONT * rows
    dims = (pts_count, grp_count, quarter, clusters)
    tall = BEFORE * rows + 8
    tail = (FRONT + BEFORE) * rows + 8 * FRONT
    shapes = (
        ((tail, rows), f32),
        ((width, width), bf16),
        ((width, width), bf16),
        ((tall, width), bf16),
        ((tall, width), bf16),
    )
    stored = call(
        functools.partial(factor_kernel, dims + (ring,)),
        [jax.ShapeDtypeStruct(*x) for x in shapes],
        (meta, front_first, tile_owner, reduced, *mine, *theirs),
        (SM, SM, SM, VM) + (VM,) * GROUP,
        [
            pltpu.VMEM((FRONT, rows, width), f32),
            pltpu.VMEM((tall, width), f32),
            pltpu.VMEM((clusters, sets * quarter, rows), f32),
            pltpu.VMEM((rows + STRIP, 2 * rows), f32),
            pltpu.VMEM((rows, 2 * rows), f32),
            pltpu.VMEM((FRONT, rows, 2 * width), f32),
            pltpu.VMEM((tall, width), f32),
        ],
        flops=400 * rows * rows * rows * 6,
    )
    return tuple(call(
        functools.partial(update_kernel, dims + (ring,)),
        [
            jax.ShapeDtypeStruct((BAND, rows, rows), f32),
            jax.ShapeDtypeStruct((1, rows), f32),
            jax.ShapeDtypeStruct((WINDOW * rows, rows), f32),
        ],
        (meta, front_first, tile_owner, reduced, *sides, *stored),
        (SM, SM, SM, VM) + (VM,) * 11,
        [
            pltpu.VMEM((BEFORE * rows, width), f32),
            pltpu.VMEM((BEFORE * rows, width), bf16),
            pltpu.VMEM((BEFORE * rows, width), bf16),
            pltpu.VMEM((clusters, sets * quarter, rows), f32),
        ],
        flops=200 * rows * rows * rows * 6,
    ))


def solution(mesh):
    in_specs = (
        P(AXES, None, None, None, None),
        P(AXES, None, None),
        P(AXES, None, None),
        P(AXES, None),
        P(),
        P(AXES, None),
        P(),
        P(),
    )
    out_specs = (P(AXES, None, None), P(AXES, None), P(None, "grp"))

    return jax.shard_map(per_device, mesh=mesh, in_specs=in_specs, out_specs=out_specs, check_vma=False)
```

profile of v0, /device:TPU:0, one launch (start us, length us, event | category | flops | bytes accessed | tf_op | source)
XLA Modules:
  0.0 129.9 jit_solution(18297715155556698042)
XLA Ops:
  0.7 1.4 %copy.15 = bf16[1,6,128,3,256]{4,2,1,3,0:T(8,128)(2,1)S(1)} copy(bf16[1,6,128,3,256]{4,2,3,1,0:T(8,128)(2,1)} %param.8) | data formatting | bytes 2359296 | tf_op args[0]
  2.1 2.6 %shard_map.103 = (f32[352,128]{1,0:T(8,128)S(1)}, f32[352,128]{1,0:T(8,128)S(1)}, f32[352,128]{1,0:T(8,128)S(1)}, f32[352,128]{1,0:T(8,128)S(1)}, f32[352,128]{1...) custom-call(s32[8]{0:T(128)S(1)} %compare_select_fusion.1.meta, ...), custom_call_target="tpu_custom_call" | custom-call | flops 528482304 | bytes 2629632 | tf_op jit(solution)/shard_map/pallas_call | solution.py:44
  5.3 2.6 %collective-permute-start.1 = (f32[352,128]{1,0:T(8,128)S(1)}, f32[352,128]{1,0:T(8,128)S(1)}, u32[]{:S(2)}, u32[]{:S(2)}) collective-permute-start(f32[352,128]{1,0:T(8,128)S(1)} %get-tuple-element.45), channel_id=1, source_target_pairs={{0,2},{1,3},{2,0},{3,1},{4,6},{5,7},{6,4},{7,5},{8,10},{9,11},{10,... | collective-permute-start | bytes 540680 | tf_op jit(solution)/shard_map/ppermute | solution.py:544
  7.9 1.8 %collective-permute-start.3 = (f32[352,128]{1,0:T(8,128)S(1)}, f32[352,128]{1,0:T(8,128)S(1)}, u32[]{:S(2)}, u32[]{:S(2)}) collective-permute-start(f32[352,128]{1,0:T(8,128)S(1)} %get-tuple-element.47), channel_id=1, source_target_pairs={{0,4},{1,5},{2,6},{3,7},{4,0},{5,1},{6,2},{7,3},{8,12},{9,13},{10,... | collective-permute-start | bytes 540680 | tf_op jit(solution)/shard_map/ppermute | solution.py:544
  9.7 2.6 %collective-permute-start.5 = (f32[352,128]{1,0:T(8,128)S(1)}, f32[352,128]{1,0:T(8,128)S(1)}, u32[]{:S(2)}, u32[]{:S(2)}) collective-permute-start(f32[352,128]{1,0:T(8,128)S(1)} %get-tuple-element.49), channel_id=1, source_target_pairs={{0,6},{1,7},{2,4},{3,5},{4,2},{5,3},{6,0},{7,1},{8,14},{9,15},{10,... | collective-permute-start | bytes 540680 | tf_op jit(solution)/shard_map/ppermute | solution.py:544
  13.3 1.6 %collective-permute-start.6 = (f32[352,128]{1,0:T(8,128)S(1)}, f32[352,128]{1,0:T(8,128)S(1)}, u32[]{:S(2)}, u32[]{:S(2)}) collective-permute-start(f32[352,128]{1,0:T(8,128)S(1)} %get-tuple-element.50), channel_id=1, source_target_pairs={{0,7},{1,6},{2,5},{3,4},{4,3},{5,2},{6,1},{7,0},{8,15},{9,14},{10,... | collective-permute-start | bytes 540680 | tf_op jit(solution)/shard_map/ppermute | solution.py:544
  14.9 1.8 %collective-permute-done.2.refs_3_ = f32[352,128]{1,0:T(8,128)S(1)} collective-permute-done((f32[352,128]{1,0:T(8,128)S(1)}, f32[352,128]{1,0:T(8,128)S(1)}, u32[]{:S(2)}, u32[]{:S(2)}) %collective-permute-start.2) | collective-permute-done | bytes 180256 | tf_op jit(solution)/shard_map/ppermute | solution.py:544
  16.7 8.9 %collective-permute-done.4.refs_5_ = f32[352,128]{1,0:T(8,128)S(1)} collective-permute-done((f32[352,128]{1,0:T(8,128)S(1)}, f32[352,128]{1,0:T(8,128)S(1)}, u32[]{:S(2)}, u32[]{:S(2)}) %collective-permute-start.4) | collective-permute-done | bytes 180256 | tf_op jit(solution)/shard_map/ppermute | solution.py:544
  25.6 2.2 %shard_map.104 = (f32[256,128]{1,0:T(8,128)S(1)}, f32[256,128]{1,0:T(8,128)S(1)}, f32[256,128]{1,0:T(8,128)S(1)}, f32[256,128]{1,0:T(8,128)S(1)}, f32[256,128]{1...) custom-call(s32[8]{0:T(128)S(1)} %copy-done.1, ...), custom_call_target="tpu_custom_call" | custom-call | bytes 2490368 | tf_op jit(solution)/shard_map/pallas_call | solution.py:44
  27.8 3.0 %collective-permute-start.10 = (f32[256,128]{1,0:T(8,128)S(1)}, f32[256,128]{1,0:T(8,128)S(1)}, u32[]{:S(2)}, u32[]{:S(2)}) collective-permute-start(f32[256,128]{1,0:T(8,128)S(1)} %get-tuple-element.55), channel_id=1, source_target_pairs={{0,16},{4,20},{8,24},{12,28},{16,0},{20,4},{24,8},{28,12},{1,17},{... | collective-permute-start | bytes 393224 | tf_op jit(solution)/shard_map/ppermute | solution.py:544
  30.8 1.3 %collective-permute-start.11 = (f32[256,128]{1,0:T(8,128)S(1)}, f32[256,128]{1,0:T(8,128)S(1)}, u32[]{:S(2)}, u32[]{:S(2)}) collective-permute-start(f32[256,128]{1,0:T(8,128)S(1)} %get-tuple-element.56), channel_id=1, source_target_pairs={{0,20},{4,16},{8,28},{12,24},{16,4},{20,0},{24,12},{28,8},{1,21},{... | collective-permute-start | bytes 393224 | tf_op jit(solution)/shard_map/ppermute | solution.py:544
  32.1 3.6 %collective-permute-start.12 = (f32[256,128]{1,0:T(8,128)S(1)}, f32[256,128]{1,0:T(8,128)S(1)}, u32[]{:S(2)}, u32[]{:S(2)}) collective-permute-start(f32[256,128]{1,0:T(8,128)S(1)} %get-tuple-element.57), channel_id=1, source_target_pairs={{0,24},{4,28},{8,16},{12,20},{16,8},{20,12},{24,0},{28,4},{1,25},{... | collective-permute-start | bytes 393224 | tf_op jit(solution)/shard_map/ppermute | solution.py:544
  35.7 1.7 %collective-permute-start.7 = (f32[256,128]{1,0:T(8,128)S(1)}, f32[256,128]{1,0:T(8,128)S(1)}, u32[]{:S(2)}, u32[]{:S(2)}) collective-permute-start(f32[256,128]{1,0:T(8,128)S(1)} %get-tuple-element.52), channel_id=1, source_target_pairs={{0,4},{4,0},{8,12},{12,8},{16,20},{20,16},{24,28},{28,24},{1,5},{5... | collective-permute-start | bytes 393224 | tf_op jit(solution)/shard_map/ppermute | solution.py:544
  37.4 9.0 %collective-permute-done.10.refs_4_ = f32[256,128]{1,0:T(8,128)S(1)} collective-permute-done((f32[256,128]{1,0:T(8,128)S(1)}, f32[256,128]{1,0:T(8,128)S(1)}, u32[]{:S(2)}, u32[]{:S(2)}) %collective-permute-start.10) | collective-permute-done | bytes 131104 | tf_op jit(solution)/shard_map/ppermute | solution.py:544
  46.9 3.6 %collective-permute-done.11.refs_5_ = f32[256,128]{1,0:T(8,128)S(1)} collective-permute-done((f32[256,128]{1,0:T(8,128)S(1)}, f32[256,128]{1,0:T(8,128)S(1)}, u32[]{:S(2)}, u32[]{:S(2)}) %collective-permute-start.11) | collective-permute-done | bytes 131104 | tf_op jit(solution)/shard_map/ppermute | solution.py:544
  51.7 4.6 %collective-permute-done.9.refs_3_ = f32[256,128]{1,0:T(8,128)S(1)} collective-permute-done((f32[256,128]{1,0:T(8,128)S(1)}, f32[256,128]{1,0:T(8,128)S(1)}, u32[]{:S(2)}, u32[]{:S(2)}) %collective-permute-start.9) | collective-permute-done | bytes 131104 | tf_op jit(solution)/shard_map/ppermute | solution.py:544
  56.3 1.4 %shard_map.105 = (f32[256,128]{1,0:T(8,128)S(1)}, f32[256,128]{1,0:T(8,128)S(1)}, f32[256,128]{1,0:T(8,128)S(1)}, f32[256,128]{1,0:T(8,128)S(1)}, f32[128,128]{1...) custom-call(s32[8]{0:T(128)S(1)} %copy-done.1, s32[8]{0:T(128)S(1)} %compare_select_fusion.1.meta, ...), custom_call_target="tpu_custom_call" | custom-call | bytes 1736704 | tf_op jit(solution)/shard_map/pallas_call | solution.py:44
  57.7 2.4 %collective-permute-start.14 = (f32[128,128]{1,0:T(8,128)S(1)}, f32[128,128]{1,0:T(8,128)S(1)}, u32[]{:S(2)}, u32[]{:S(2)}) collective-permute-start(f32[128,128]{1,0:T(8,128)S(1)} %get-tuple-element.60), channel_id=1, source_target_pairs={{0,8},{1,9},{2,10},{3,11},{4,12},{5,13},{6,14},{7,15},{8,16},{9,17... | collective-permute-start | bytes 196616 | tf_op jit(solution)/shard_map/ppermute | solution.py:622
  60.1 2.0 %collective-permute-start.15 = (f32[128,128]{1,0:T(8,128)S(1)}, f32[128,128]{1,0:T(8,128)S(1)}, u32[]{:S(2)}, u32[]{:S(2)}) collective-permute-start(f32[128,128]{1,0:T(8,128)S(1)} %get-tuple-element.60), channel_id=1, source_target_pairs={{0,16},{1,17},{2,18},{3,19},{4,20},{5,21},{6,22},{7,23},{8,24},{9,... | collective-permute-start | bytes 196616 | tf_op jit(solution)/shard_map/ppermute | solution.py:622
  62.1 2.8 %collective-permute-start.16 = (f32[128,128]{1,0:T(8,128)S(1)}, f32[128,128]{1,0:T(8,128)S(1)}, u32[]{:S(2)}, u32[]{:S(2)}) collective-permute-start(f32[128,128]{1,0:T(8,128)S(1)} %get-tuple-element.60), channel_id=1, source_target_pairs={{0,24},{1,25},{2,26},{3,27},{4,28},{5,29},{6,30},{7,31},{8,0},{9,1... | collective-permute-start | bytes 196616 | tf_op jit(solution)/shard_map/ppermute | solution.py:622
  64.9 1.4 %collective-permute-done.15 = f32[128,128]{1,0:T(8,128)S(1)} collective-permute-done((f32[128,128]{1,0:T(8,128)S(1)}, f32[128,128]{1,0:T(8,128)S(1)}, u32[]{:S(2)}, u32[]{:S(2)}) %collective-permute-start.15) | collective-permute-done | bytes 65568 | tf_op jit(solution)/shard_map/ppermute | solution.py:622
  67.1 1.2 collective-permute-start.17
  68.2 3.7 %collective-permute-start.18 = (f32[128,128]{1,0:T(8,128)S(1)}, f32[128,128]{1,0:T(8,128)S(1)}, u32[]{:S(2)}, u32[]{:S(2)}) collective-permute-start(f32[128,128]{1,0:T(8,128)S(1)} %get-tuple-element.66), channel_id=1, source_target_pairs={{0,16},{1,17},{2,18},{3,19},{4,20},{5,21},{6,22},{7,23},{8,24},{9,... | collective-permute-start | bytes 196616 | tf_op jit(solution)/shard_map/ppermute | solution.py:622
  72.0 1.7 %collective-permute-done.17 = f32[128,128]{1,0:T(8,128)S(1)} collective-permute-done((f32[128,128]{1,0:T(8,128)S(1)}, f32[128,128]{1,0:T(8,128)S(1)}, u32[]{:S(2)}, u32[]{:S(2)}) %collective-permute-start.17) | collective-permute-done | bytes 65568 | tf_op jit(solution)/shard_map/ppermute | solution.py:622
  73.7 1.4 %collective-permute-done.18 = f32[128,128]{1,0:T(8,128)S(1)} collective-permute-done((f32[128,128]{1,0:T(8,128)S(1)}, f32[128,128]{1,0:T(8,128)S(1)}, u32[]{:S(2)}, u32[]{:S(2)}) %collective-permute-start.18) | collective-permute-done | bytes 65568 | tf_op jit(solution)/shard_map/ppermute | solution.py:622
  75.1 1.2 collective-permute-done.19
  76.4 1.6 %collective-permute-start.21 = (f32[512,128]{1,0:T(8,128)S(1)}, f32[512,128]{1,0:T(8,128)S(1)}, u32[]{:S(2)}, u32[]{:S(2)}) collective-permute-start(f32[512,128]{1,0:T(8,128)S(1)} %pad_maximum_fusion.refs_0_), channel_id=1, source_target_pairs={{0,2},{1,3},{2,0},{3,1},{4,6},{5,7},{6,4},{7,5},{8,10},{9,11},{10,... | collective-permute-start | bytes 786440 | tf_op jit(solution)/shard_map/ppermute | solution.py:629
  80.0 5.6 %collective-permute-done.21.refs_1_ = f32[512,128]{1,0:T(8,128)S(1)} collective-permute-done((f32[512,128]{1,0:T(8,128)S(1)}, f32[512,128]{1,0:T(8,128)S(1)}, u32[]{:S(2)}, u32[]{:S(2)}) %collective-permute-start.21) | collective-permute-done | bytes 262176 | tf_op jit(solution)/shard_map/ppermute | solution.py:629
  85.7 6.3 %collective-permute-done.22.refs_2_ = f32[512,128]{1,0:T(8,128)S(1)} collective-permute-done((f32[512,128]{1,0:T(8,128)S(1)}, f32[512,128]{1,0:T(8,128)S(1)}, u32[]{:S(2)}, u32[]{:S(2)}) %collective-permute-start.22) | collective-permute-done | bytes 262176 | tf_op jit(solution)/shard_map/ppermute | solution.py:629
  94.2 1.7 %collective-permute-start.26 = (f32[1024,128]{1,0:T(8,128)S(1)}, f32[1024,128]{1,0:T(8,128)S(1)}, u32[]{:S(2)}, u32[]{:S(2)}) collective-permute-start(f32[1024,128]{1,0:T(8,128)S(1)} %get-tuple-element.72), channel_id=1, source_target_pairs={{0,6},{1,7},{2,4},{3,5},{4,2},{5,3},{6,0},{7,1},{8,14},{9,15},{10,... | collective-permute-start | bytes 1572872 | tf_op jit(solution)/shard_map/ppermute | solution.py:629
  96.0 30.3 %shard_map.106 = (f32[1440,128]{1,0:T(8,128)S(1)}, bf16[512,512]{1,0:T(8,128)(2,1)S(1)}, bf16[512,512]{1,0:T(8,128)(2,1)S(1)}, bf16[904,512]{1,0:T(8,128)(2,1)S(1)}, bf16[904,512]{1,0:T(8,128)(2,1)S(1)}) custom-call(s32[8]{0:T(128)S(1)} %compare_select_fusion.1.meta, s32[1]{0:T(128)S(6)} %copy.29.front, s32[8]{0:T(128)S(1)} %copy-done.1, ...), custom_call_target="tpu_custom_call" | custom-call | flops 5033164800 | bytes 5750784 | tf_op jit(solution)/shard_map/pallas_call | solution.py:44
  126.4 3.5 %shard_map.107 = (f32[8,128,128]{2,1,0:T(8,128)}, f32[1,128]{1,0:T(1,128)}, f32[2304,128]{1,0:T(8,128)}) custom-call(s32[8]{0:T(128)S(1)} %compare_select_fusion.1.meta, s32[1]{0:T(128)S(6)} %copy.29.front, s32[8]{0:T(128)S(1)} %copy-done.1, f32[32,128]{1,0:T(8,128)S(1)} %get-tuple-element.59.reduced, f32[512,128]{1,0:T(8,128)S(1)} %pad_maximum_fusion.1.refs_0_, ...), custom_call_target="tpu_custom_call" | custom-call | flops 2516582400 | bytes 8110592 | tf_op jit(solution)/shard_map/pallas_call | solution.py:44
  (62 shorter events, 8.0 us)
Async XLA Ops:
  4.7 51.6 %copy-start = (f32[32,128]{1,0:T(8,128)S(1)}, f32[32,128]{1,0:T(8,128)}, u32[]{:S(2)}) copy-start(f32[32,128]{1,0:T(8,128)} %damping.1) | copy-start | bytes 49156
  4.8 4.9 %collective-permute-start = (f32[352,128]{1,0:T(8,128)S(1)}, f32[352,128]{1,0:T(8,128)S(1)}, u32[]{:S(2)}, u32[]{:S(2)}) collective-permute-start(f32[352,128]{1,0:T(8,128)S(1)} %get-tuple-element.44), channel_id=1, source_target_pairs={{0,1},{1,0},{2,3},{3,2},{4,5},{5,4},{6,7},{7,6},{8,9},{9,8},{10,11... | collective-permute-start | bytes 540680 | tf_op jit(solution)/shard_map/ppermute | solution.py:544
  5.3 8.0 %collective-permute-start.1 = (f32[352,128]{1,0:T(8,128)S(1)}, f32[352,128]{1,0:T(8,128)S(1)}, u32[]{:S(2)}, u32[]{:S(2)}) collective-permute-start(f32[352,128]{1,0:T(8,128)S(1)} %get-tuple-element.45), channel_id=1, source_target_pairs={{0,2},{1,3},{2,0},{3,1},{4,6},{5,7},{6,4},{7,5},{8,10},{9,11},{10,... | collective-permute-start | bytes 540680 | tf_op jit(solution)/shard_map/ppermute | solution.py:544
  7.9 8.8 %collective-permute-start.2 = (f32[352,128]{1,0:T(8,128)S(1)}, f32[352,128]{1,0:T(8,128)S(1)}, u32[]{:S(2)}, u32[]{:S(2)}) collective-permute-start(f32[352,128]{1,0:T(8,128)S(1)} %get-tuple-element.46), channel_id=1, source_target_pairs={{0,3},{1,2},{2,1},{3,0},{4,7},{5,6},{6,5},{7,4},{8,11},{9,10},{10,... | collective-permute-start | bytes 540680 | tf_op jit(solution)/shard_map/ppermute | solution.py:544
  7.9 8.8 %collective-permute-start.3 = (f32[352,128]{1,0:T(8,128)S(1)}, f32[352,128]{1,0:T(8,128)S(1)}, u32[]{:S(2)}, u32[]{:S(2)}) collective-permute-start(f32[352,128]{1,0:T(8,128)S(1)} %get-tuple-element.47), channel_id=1, source_target_pairs={{0,4},{1,5},{2,6},{3,7},{4,0},{5,1},{6,2},{7,3},{8,12},{9,13},{10,... | collective-permute-start | bytes 540680 | tf_op jit(solution)/shard_map/ppermute | solution.py:544
  9.7 15.9 %collective-permute-start.4 = (f32[352,128]{1,0:T(8,128)S(1)}, f32[352,128]{1,0:T(8,128)S(1)}, u32[]{:S(2)}, u32[]{:S(2)}) collective-permute-start(f32[352,128]{1,0:T(8,128)S(1)} %get-tuple-element.48), channel_id=1, source_target_pairs={{0,5},{1,4},{2,7},{3,6},{4,1},{5,0},{6,3},{7,2},{8,13},{9,12},{10,... | collective-permute-start | bytes 540680 | tf_op jit(solution)/shard_map/ppermute | solution.py:544
  9.7 15.9 %collective-permute-start.5 = (f32[352,128]{1,0:T(8,128)S(1)}, f32[352,128]{1,0:T(8,128)S(1)}, u32[]{:S(2)}, u32[]{:S(2)}) collective-permute-start(f32[352,128]{1,0:T(8,128)S(1)} %get-tuple-element.49), channel_id=1, source_target_pairs={{0,6},{1,7},{2,4},{3,5},{4,2},{5,3},{6,0},{7,1},{8,14},{9,15},{10,... | collective-permute-start | bytes 540680 | tf_op jit(solution)/shard_map/ppermute | solution.py:544
  13.3 12.3 %collective-permute-start.6 = (f32[352,128]{1,0:T(8,128)S(1)}, f32[352,128]{1,0:T(8,128)S(1)}, u32[]{:S(2)}, u32[]{:S(2)}) collective-permute-start(f32[352,128]{1,0:T(8,128)S(1)} %get-tuple-element.50), channel_id=1, source_target_pairs={{0,7},{1,6},{2,5},{3,4},{4,3},{5,2},{6,1},{7,0},{8,15},{9,14},{10,... | collective-permute-start | bytes 540680 | tf_op jit(solution)/shard_map/ppermute | solution.py:544
  27.8 18.6 %collective-permute-start.10 = (f32[256,128]{1,0:T(8,128)S(1)}, f32[256,128]{1,0:T(8,128)S(1)}, u32[]{:S(2)}, u32[]{:S(2)}) collective-permute-start(f32[256,128]{1,0:T(8,128)S(1)} %get-tuple-element.55), channel_id=1, source_target_pairs={{0,16},{4,20},{8,24},{12,28},{16,0},{20,4},{24,8},{28,12},{1,17},{... | collective-permute-start | bytes 393224 | tf_op jit(solution)/shard_map/ppermute | solution.py:544
  30.8 19.7 %collective-permute-start.11 = (f32[256,128]{1,0:T(8,128)S(1)}, f32[256,128]{1,0:T(8,128)S(1)}, u32[]{:S(2)}, u32[]{:S(2)}) collective-permute-start(f32[256,128]{1,0:T(8,128)S(1)} %get-tuple-element.56), channel_id=1, source_target_pairs={{0,20},{4,16},{8,28},{12,24},{16,4},{20,0},{24,12},{28,8},{1,21},{... | collective-permute-start | bytes 393224 | tf_op jit(solution)/shard_map/ppermute | solution.py:544
  32.1 19.2 %collective-permute-start.12 = (f32[256,128]{1,0:T(8,128)S(1)}, f32[256,128]{1,0:T(8,128)S(1)}, u32[]{:S(2)}, u32[]{:S(2)}) collective-permute-start(f32[256,128]{1,0:T(8,128)S(1)} %get-tuple-element.57), channel_id=1, source_target_pairs={{0,24},{4,28},{8,16},{12,20},{16,8},{20,12},{24,0},{28,4},{1,25},{... | collective-permute-start | bytes 393224 | tf_op jit(solution)/shard_map/ppermute | solution.py:544
  35.7 15.6 %collective-permute-start.13 = (f32[256,128]{1,0:T(8,128)S(1)}, f32[256,128]{1,0:T(8,128)S(1)}, u32[]{:S(2)}, u32[]{:S(2)}) collective-permute-start(f32[256,128]{1,0:T(8,128)S(1)} %get-tuple-element.58), channel_id=1, source_target_pairs={{0,28},{4,24},{8,20},{12,16},{16,12},{20,8},{24,4},{28,0},{1,29},{... | collective-permute-start | bytes 393224 | tf_op jit(solution)/shard_map/ppermute | solution.py:544
  35.7 15.6 %collective-permute-start.7 = (f32[256,128]{1,0:T(8,128)S(1)}, f32[256,128]{1,0:T(8,128)S(1)}, u32[]{:S(2)}, u32[]{:S(2)}) collective-permute-start(f32[256,128]{1,0:T(8,128)S(1)} %get-tuple-element.52), channel_id=1, source_target_pairs={{0,4},{4,0},{8,12},{12,8},{16,20},{20,16},{24,28},{28,24},{1,5},{5... | collective-permute-start | bytes 393224 | tf_op jit(solution)/shard_map/ppermute | solution.py:544
  46.4 5.4 %collective-permute-start.8 = (f32[256,128]{1,0:T(8,128)S(1)}, f32[256,128]{1,0:T(8,128)S(1)}, u32[]{:S(2)}, u32[]{:S(2)}) collective-permute-start(f32[256,128]{1,0:T(8,128)S(1)} %get-tuple-element.53), channel_id=1, source_target_pairs={{0,8},{4,12},{8,0},{12,4},{16,24},{20,28},{24,16},{28,20},{1,9},{5... | collective-permute-start | bytes 393224 | tf_op jit(solution)/shard_map/ppermute | solution.py:544
  50.5 5.9 %collective-permute-start.9 = (f32[256,128]{1,0:T(8,128)S(1)}, f32[256,128]{1,0:T(8,128)S(1)}, u32[]{:S(2)}, u32[]{:S(2)}) collective-permute-start(f32[256,128]{1,0:T(8,128)S(1)} %get-tuple-element.54), channel_id=1, source_target_pairs={{0,12},{4,8},{8,4},{12,0},{16,28},{20,24},{24,20},{28,16},{1,13},{... | collective-permute-start | bytes 393224 | tf_op jit(solution)/shard_map/ppermute | solution.py:544
  57.7 7.2 %collective-permute-start.14 = (f32[128,128]{1,0:T(8,128)S(1)}, f32[128,128]{1,0:T(8,128)S(1)}, u32[]{:S(2)}, u32[]{:S(2)}) collective-permute-start(f32[128,128]{1,0:T(8,128)S(1)} %get-tuple-element.60), channel_id=1, source_target_pairs={{0,8},{1,9},{2,10},{3,11},{4,12},{5,13},{6,14},{7,15},{8,16},{9,17... | collective-permute-start | bytes 196616 | tf_op jit(solution)/shard_map/ppermute | solution.py:622
  60.1 6.2 %collective-permute-start.15 = (f32[128,128]{1,0:T(8,128)S(1)}, f32[128,128]{1,0:T(8,128)S(1)}, u32[]{:S(2)}, u32[]{:S(2)}) collective-permute-start(f32[128,128]{1,0:T(8,128)S(1)} %get-tuple-element.60), channel_id=1, source_target_pairs={{0,16},{1,17},{2,18},{3,19},{4,20},{5,21},{6,22},{7,23},{8,24},{9,... | collective-permute-start | bytes 196616 | tf_op jit(solution)/shard_map/ppermute | solution.py:622
  62.1 5.0 %collective-permute-start.16 = (f32[128,128]{1,0:T(8,128)S(1)}, f32[128,128]{1,0:T(8,128)S(1)}, u32[]{:S(2)}, u32[]{:S(2)}) collective-permute-start(f32[128,128]{1,0:T(8,128)S(1)} %get-tuple-element.60), channel_id=1, source_target_pairs={{0,24},{1,25},{2,26},{3,27},{4,28},{5,29},{6,30},{7,31},{8,0},{9,1... | collective-permute-start | bytes 196616 | tf_op jit(solution)/shard_map/ppermute | solution.py:622
  67.1 6.6 %collective-permute-start.17 = (f32[128,128]{1,0:T(8,128)S(1)}, f32[128,128]{1,0:T(8,128)S(1)}, u32[]{:S(2)}, u32[]{:S(2)}) collective-permute-start(f32[128,128]{1,0:T(8,128)S(1)} %get-tuple-element.66), channel_id=1, source_target_pairs={{0,8},{1,9},{2,10},{3,11},{4,12},{5,13},{6,14},{7,15},{8,16},{9,17... | collective-permute-start | bytes 196616 | tf_op jit(solution)/shard_map/ppermute | solution.py:622
  68.2 6.8 %collective-permute-start.18 = (f32[128,128]{1,0:T(8,128)S(1)}, f32[128,128]{1,0:T(8,128)S(1)}, u32[]{:S(2)}, u32[]{:S(2)}) collective-permute-start(f32[128,128]{1,0:T(8,128)S(1)} %get-tuple-element.66), channel_id=1, source_target_pairs={{0,16},{1,17},{2,18},{3,19},{4,20},{5,21},{6,22},{7,23},{8,24},{9,... | collective-permute-start | bytes 196616 | tf_op jit(solution)/shard_map/ppermute | solution.py:622
  72.0 4.3 %collective-permute-start.19 = (f32[128,128]{1,0:T(8,128)S(1)}, f32[128,128]{1,0:T(8,128)S(1)}, u32[]{:S(2)}, u32[]{:S(2)}) collective-permute-start(f32[128,128]{1,0:T(8,128)S(1)} %get-tuple-element.66), channel_id=1, source_target_pairs={{0,24},{1,25},{2,26},{3,27},{4,28},{5,29},{6,30},{7,31},{8,0},{9,1... | collective-permute-start | bytes 196616 | tf_op jit(solution)/shard_map/ppermute | solution.py:622
  76.3 3.6 %collective-permute-start.20 = (f32[1024,128]{1,0:T(8,128)S(1)}, f32[1024,128]{1,0:T(8,128)S(1)}, u32[]{:S(2)}, u32[]{:S(2)}) collective-permute-start(f32[1024,128]{1,0:T(8,128)S(1)} %constant_dynamic-update-slice_fusion), channel_id=1, source_target_pairs={{0,1},{1,0},{2,3},{3,2},{4,5},{5,4},{6,7},{7,6},{8,9},{9,8},{10,11... | collective-permute-start | bytes 1572872 | tf_op jit(solution)/shard_map/ppermute | solution.py:637
  76.4 9.2 %collective-permute-start.21 = (f32[512,128]{1,0:T(8,128)S(1)}, f32[512,128]{1,0:T(8,128)S(1)}, u32[]{:S(2)}, u32[]{:S(2)}) collective-permute-start(f32[512,128]{1,0:T(8,128)S(1)} %pad_maximum_fusion.refs_0_), channel_id=1, source_target_pairs={{0,2},{1,3},{2,0},{3,1},{4,6},{5,7},{6,4},{7,5},{8,10},{9,11},{10,... | collective-permute-start | bytes 786440 | tf_op jit(solution)/shard_map/ppermute | solution.py:629
  78.0 14.0 %collective-permute-start.22 = (f32[512,128]{1,0:T(8,128)S(1)}, f32[512,128]{1,0:T(8,128)S(1)}, u32[]{:S(2)}, u32[]{:S(2)}) collective-permute-start(f32[512,128]{1,0:T(8,128)S(1)} %pad_maximum_fusion.refs_0_), channel_id=1, source_target_pairs={{0,4},{1,5},{2,6},{3,7},{4,0},{5,1},{6,2},{7,3},{8,12},{9,13},{10,... | collective-permute-start | bytes 786440 | tf_op jit(solution)/shard_map/ppermute | solution.py:629
  79.1 12.9 %collective-permute-start.23 = (f32[512,128]{1,0:T(8,128)S(1)}, f32[512,128]{1,0:T(8,128)S(1)}, u32[]{:S(2)}, u32[]{:S(2)}) collective-permute-start(f32[512,128]{1,0:T(8,128)S(1)} %pad_maximum_fusion.refs_0_), channel_id=1, source_target_pairs={{0,6},{1,7},{2,4},{3,5},{4,2},{5,3},{6,0},{7,1},{8,14},{9,15},{10,... | collective-permute-start | bytes 786440 | tf_op jit(solution)/shard_map/ppermute | solution.py:629
  80.0 13.3 %collective-permute-start.27 = (f32[512,128]{1,0:T(8,128)S(1)}, f32[512,128]{1,0:T(8,128)S(1)}, u32[]{:S(2)}, u32[]{:S(2)}) collective-permute-start(f32[512,128]{1,0:T(8,128)S(1)} %pad_maximum_fusion.refs_0_), channel_id=1, source_target_pairs={{0,1},{1,0},{2,3},{3,2},{4,5},{5,4},{6,7},{7,6},{8,9},{9,8},{10,11... | collective-permute-start | bytes 786440 | tf_op jit(solution)/shard_map/ppermute | solution.py:635
  92.0 2.3 %collective-permute-start.28 = (f32[512,128]{1,0:T(8,128)S(1)}, f32[512,128]{1,0:T(8,128)S(1)}, u32[]{:S(2)}, u32[]{:S(2)}) collective-permute-start(f32[512,128]{1,0:T(8,128)S(1)} %collective-permute-done.21.refs_1_), channel_id=1, source_target_pairs={{0,1},{1,0},{2,3},{3,2},{4,5},{5,4},{6,7},{7,6},{8,9},{9,8},{10,11... | collective-permute-start | bytes 786440 | tf_op jit(solution)/shard_map/ppermute | solution.py:643
  92.0 34.4 %collective-permute-start.24 = (f32[1536,128]{1,0:T(8,128)S(1)}, f32[1536,128]{1,0:T(8,128)S(1)}, u32[]{:S(2)}, u32[]{:S(2)}) collective-permute-start(f32[1536,128]{1,0:T(8,128)S(1)} %slice_dynamic-update-slice_fusion.2), channel_id=1, source_target_pairs={{0,2},{1,3},{2,0},{3,1},{4,6},{5,7},{6,4},{7,5},{8,10},{9,11},{10,... | collective-permute-start | bytes 2359304 | tf_op jit(solution)/shard_map/ppermute | solution.py:629
  92.8 3.2 %collective-permute-start.29 = (f32[512,128]{1,0:T(8,128)S(1)}, f32[512,128]{1,0:T(8,128)S(1)}, u32[]{:S(2)}, u32[]{:S(2)}) collective-permute-start(f32[512,128]{1,0:T(8,128)S(1)} %collective-permute-done.22.refs_2_), channel_id=1, source_target_pairs={{0,1},{1,0},{2,3},{3,2},{4,5},{5,4},{6,7},{7,6},{8,9},{9,8},{10,11... | collective-permute-start | bytes 786440 | tf_op jit(solution)/shard_map/ppermute | solution.py:643
  93.0 3.0 %collective-permute-start.30 = (f32[512,128]{1,0:T(8,128)S(1)}, f32[512,128]{1,0:T(8,128)S(1)}, u32[]{:S(2)}, u32[]{:S(2)}) collective-permute-start(f32[512,128]{1,0:T(8,128)S(1)} %collective-permute-done.23.refs_3_), channel_id=1, source_target_pairs={{0,1},{1,0},{2,3},{3,2},{4,5},{5,4},{6,7},{7,6},{8,9},{9,8},{10,11... | collective-permute-start | bytes 786440 | tf_op jit(solution)/shard_map/ppermute | solution.py:643
  93.3 33.1 %collective-permute-start.25 = (f32[1024,128]{1,0:T(8,128)S(1)}, f32[1024,128]{1,0:T(8,128)S(1)}, u32[]{:S(2)}, u32[]{:S(2)}) collective-permute-start(f32[1024,128]{1,0:T(8,128)S(1)} %get-tuple-element.72), channel_id=1, source_target_pairs={{0,4},{1,5},{2,6},{3,7},{4,0},{5,1},{6,2},{7,3},{8,12},{9,13},{10,... | collective-permute-start | bytes 1572872 | tf_op jit(solution)/shard_map/ppermute | solution.py:629
  94.2 32.1 %collective-permute-start.26 = (f32[1024,128]{1,0:T(8,128)S(1)}, f32[1024,128]{1,0:T(8,128)S(1)}, u32[]{:S(2)}, u32[]{:S(2)}) collective-permute-start(f32[1024,128]{1,0:T(8,128)S(1)} %get-tuple-element.72), channel_id=1, source_target_pairs={{0,6},{1,7},{2,4},{3,5},{4,2},{5,3},{6,0},{7,1},{8,14},{9,15},{10,... | collective-permute-start | bytes 1572872 | tf_op jit(solution)/shard_map/ppermute | solution.py:629
  (5 other events, 29.3 us)
where the time goes:
time: 130 us
  waiting for transfers between devices  47.6 us (37%)
  Pallas kernels  40 us (31%)
  starting transfers between devices  39.2 us (30%)
  between operations  1.59 us (1%)
  local copies, waits for them, and re-layouts  1.58 us (1%)
    pallas_call x5, Pallas kernels, call(): pl.pallas_call(kernel, out_shape=out_shapes, in_specs=[spec(s) for s in s...  40 us
    ppermute x14, waiting for transfers between devices, flip(): lax.ppermute(value, axis, [(p, p ^ bit + 1) for p in range(count)])  29.3 us
    ppermute x14, starting transfers between devices, flip(): lax.ppermute(value, axis, [(p, p ^ bit + 1) for p in range(count)])  19.4 us
    ppermute x6, starting transfers between devices, along(): moved.append(lax.ppermute(value, AXES, pairs))  12.1 us
    ppermute x6, waiting for transfers between devices, across(): moved.append(lax.ppermute(value, AXES, pairs))  11.9 us
    ppermute x6, starting transfers between devices, across(): moved.append(lax.ppermute(value, AXES, pairs))  7.04 us
    ppermute x6, waiting for transfers between devices, along(): moved.append(lax.ppermute(value, AXES, pairs))  6.35 us
  transfers between devices with their start and end apart: 31, of which 14 were waited for; matrix products, arithmetic and copies ran while one was open for 0% of the time, Pallas kernels for 23%

commit v1 on v0

--- a/solution.py
+++ b/solution.py
@@ -372,15 +372,14 @@
         at = pl.multiple_of(p * STRIP, STRIP)
         lhs = jnp.where(lanes >= at + STRIP, past[:, 0:rows], 0.0)
         work[0:rows, :] = work[0:rows, :] - product3(halves(lhs), halves(past), TN)
-        ahead = work[pl.ds(at + STRIP, STRIP), :]
         now_a, now_i = now[:, 0:rows], now[:, rows : 2 * rows]
-        next_a, next_i = ahead[:, 0:rows], ahead[:, rows : 2 * rows]
         shift = lax.rem(rows - at, rows)
         turned = pltpu.roll(now_a, shift, 1)
-        turned_next = pltpu.roll(next_a, shift, 1)
+        turned_next = turned.T[STRIP : 2 * STRIP, :]
         column = [jnp.broadcast_to(turned[:, i : i + 1], (STRIP, rows)) for i in range(STRIP)]
         below = [jnp.broadcast_to(turned_next[:, i : i + 1], (STRIP, rows)) for i in range(STRIP)]
         norm = jnp.zeros((STRIP, rows), jnp.float32)
+        next_a, next_i = norm, norm
 
         def row(value, i):
             return jnp.broadcast_to(value[i : i + 1, :], (STRIP, rows))
@@ -407,11 +406,12 @@
             low_i = row(now_i, i + 1) - ratio * line_i
             now_a = now_a - scale * line_a - second * low_a
             now_i = now_i - scale * line_i - second * low_i
-            next_a = next_a - scale_next * line_a - second_next * low_a
-            next_i = next_i - scale_next * line_i - second_next * low_i
+            next_a = next_a + (scale_next * line_a + second_next * low_a)
+            next_i = next_i + (scale_next * line_i + second_next * low_i)
         finished = jnp.concatenate([now_a * norm, now_i * norm], axis=1)
         done[pl.ds(at, STRIP), :] = finished
-        return (jnp.concatenate([next_a, next_i], axis=1), finished)
+        ahead = work[pl.ds(at + STRIP, STRIP), :]
+        return (ahead - jnp.concatenate([next_a, next_i], axis=1), finished)
 
     first = work[0:STRIP, :]
     lax.fori_loop(0, rows // STRIP, strip, (first, jnp.zeros_like(first)))

time: 130 us -> 128 us (0.985)
  Pallas kernels: 40 us -> 35.1 us
  waiting for transfers between devices: 47.6 us -> 49.9 us
    pallas_call x5, Pallas kernels: 40 us -> 35.1 us  [call(): pl.pallas_call(kernel, out_shape=out_shapes, in_specs=[spec(s) for s in s...]
    ppermute x6, waiting for transfers between devices: 11.9 us -> 14.3 us  [across(): moved.append(lax.ppermute(value, AXES, pairs))]
  transfers between devices with their start and end apart: 31 -> 31, of which waited for: 14 -> 15; matrix products, arithmetic and copies ran while one was open for 0% -> 0% of each run, Pallas kernels for 23% -> 20%
where the time goes in v1:
time: 128 us; the launch traced here: 127 us
  waiting for transfers between devices  49.9 us (39%)
  starting transfers between devices  39.2 us (31%)
  Pallas kernels  35.1 us (27%)
  local copies, waits for them, and re-layouts  1.58 us (1%)
  between operations  1.57 us (1%)
    pallas_call x5, Pallas kernels, call(): pl.pallas_call(kernel, out_shape=out_shapes, in_specs=[spec(s) for s in s...  35.1 us
    ppermute x14, waiting for transfers between devices, flip(): lax.ppermute(value, axis, [(p, p ^ bit + 1) for p in range(count)])  29.3 us
    ppermute x14, starting transfers between devices, flip(): lax.ppermute(value, axis, [(p, p ^ bit + 1) for p in range(count)])  19.4 us
    ppermute x6, waiting for transfers between devices, across(): moved.append(lax.ppermute(value, AXES, pairs))  14.3 us
    ppermute x6, starting transfers between devices, along(): moved.append(lax.ppermute(value, AXES, pairs))  12.1 us
    ppermute x6, starting transfers between devices, across(): moved.append(lax.ppermute(value, AXES, pairs))  7.04 us
    ppermute x6, waiting for transfers between devices, along(): moved.append(lax.ppermute(value, AXES, pairs))  6.35 us
  transfers between devices with their start and end apart: 31, of which 15 were waited for; matrix products, arithmetic and copies ran while one was open for 0% of the time, Pallas kernels for 20%

profile of v1, /device:TPU:0, one launch (start us, length us, event | category | flops | bytes accessed | tf_op | source)
XLA Modules:
  0.0 127.4 jit_solution(15473144342513368638)
XLA Ops:
  0.7 1.4 %copy.15 = bf16[1,6,128,3,256]{4,2,1,3,0:T(8,128)(2,1)S(1)} copy(bf16[1,6,128,3,256]{4,2,3,1,0:T(8,128)(2,1)} %param.8) | data formatting | bytes 2359296 | tf_op args[0]
  2.1 2.6 %shard_map.103 = (f32[352,128]{1,0:T(8,128)S(1)}, f32[352,128]{1,0:T(8,128)S(1)}, f32[352,128]{1,0:T(8,128)S(1)}, f32[352,128]{1,0:T(8,128)S(1)}, f32[352,128]{1...) custom-call(s32[8]{0:T(128)S(1)} %compare_select_fusion.1.meta, ...), custom_call_target="tpu_custom_call" | custom-call | flops 528482304 | bytes 2629632 | tf_op jit(solution)/shard_map/pallas_call | solution.py:44
  5.3 2.6 %collective-permute-start.1 = (f32[352,128]{1,0:T(8,128)S(1)}, f32[352,128]{1,0:T(8,128)S(1)}, u32[]{:S(2)}, u32[]{:S(2)}) collective-permute-start(f32[352,128]{1,0:T(8,128)S(1)} %get-tuple-element.45), channel_id=1, source_target_pairs={{0,2},{1,3},{2,0},{3,1},{4,6},{5,7},{6,4},{7,5},{8,10},{9,11},{10,... | collective-permute-start | bytes 540680 | tf_op jit(solution)/shard_map/ppermute | solution.py:544
  7.9 1.8 %collective-permute-start.3 = (f32[352,128]{1,0:T(8,128)S(1)}, f32[352,128]{1,0:T(8,128)S(1)}, u32[]{:S(2)}, u32[]{:S(2)}) collective-permute-start(f32[352,128]{1,0:T(8,128)S(1)} %get-tuple-element.47), channel_id=1, source_target_pairs={{0,4},{1,5},{2,6},{3,7},{4,0},{5,1},{6,2},{7,3},{8,12},{9,13},{10,... | collective-permute-start | bytes 540680 | tf_op jit(solution)/shard_map/ppermute | solution.py:544
  9.7 2.6 %collective-permute-start.5 = (f32[352,128]{1,0:T(8,128)S(1)}, f32[352,128]{1,0:T(8,128)S(1)}, u32[]{:S(2)}, u32[]{:S(2)}) collective-permute-start(f32[352,128]{1,0:T(8,128)S(1)} %get-tuple-element.49), channel_id=1, source_target_pairs={{0,6},{1,7},{2,4},{3,5},{4,2},{5,3},{6,0},{7,1},{8,14},{9,15},{10,... | collective-permute-start | bytes 540680 | tf_op jit(solution)/shard_map/ppermute | solution.py:544
  13.3 1.6 %collective-permute-start.6 = (f32[352,128]{1,0:T(8,128)S(1)}, f32[352,128]{1,0:T(8,128)S(1)}, u32[]{:S(2)}, u32[]{:S(2)}) collective-permute-start(f32[352,128]{1,0:T(8,128)S(1)} %get-tuple-element.50), channel_id=1, source_target_pairs={{0,7},{1,6},{2,5},{3,4},{4,3},{5,2},{6,1},{7,0},{8,15},{9,14},{10,... | collective-permute-start | bytes 540680 | tf_op jit(solution)/shard_map/ppermute | solution.py:544
  14.9 1.8 %collective-permute-done.2.refs_3_ = f32[352,128]{1,0:T(8,128)S(1)} collective-permute-done((f32[352,128]{1,0:T(8,128)S(1)}, f32[352,128]{1,0:T(8,128)S(1)}, u32[]{:S(2)}, u32[]{:S(2)}) %collective-permute-start.2) | collective-permute-done | bytes 180256 | tf_op jit(solution)/shard_map/ppermute | solution.py:544
  16.7 8.9 %collective-permute-done.4.refs_5_ = f32[352,128]{1,0:T(8,128)S(1)} collective-permute-done((f32[352,128]{1,0:T(8,128)S(1)}, f32[352,128]{1,0:T(8,128)S(1)}, u32[]{:S(2)}, u32[]{:S(2)}) %collective-permute-start.4) | collective-permute-done | bytes 180256 | tf_op jit(solution)/shard_map/ppermute | solution.py:544
  25.6 2.2 %shard_map.104 = (f32[256,128]{1,0:T(8,128)S(1)}, f32[256,128]{1,0:T(8,128)S(1)}, f32[256,128]{1,0:T(8,128)S(1)}, f32[256,128]{1,0:T(8,128)S(1)}, f32[256,128]{1...) custom-call(s32[8]{0:T(128)S(1)} %copy-done.1, ...), custom_call_target="tpu_custom_call" | custom-call | bytes 2490368 | tf_op jit(solution)/shard_map/pallas_call | solution.py:44
  27.8 3.0 %collective-permute-start.10 = (f32[256,128]{1,0:T(8,128)S(1)}, f32[256,128]{1,0:T(8,128)S(1)}, u32[]{:S(2)}, u32[]{:S(2)}) collective-permute-start(f32[256,128]{1,0:T(8,128)S(1)} %get-tuple-element.55), channel_id=1, source_target_pairs={{0,16},{4,20},{8,24},{12,28},{16,0},{20,4},{24,8},{28,12},{1,17},{... | collective-permute-start | bytes 393224 | tf_op jit(solution)/shard_map/ppermute | solution.py:544
  30.8 1.3 %collective-permute-start.11 = (f32[256,128]{1,0:T(8,128)S(1)}, f32[256,128]{1,0:T(8,128)S(1)}, u32[]{:S(2)}, u32[]{:S(2)}) collective-permute-start(f32[256,128]{1,0:T(8,128)S(1)} %get-tuple-element.56), channel_id=1, source_target_pairs={{0,20},{4,16},{8,28},{12,24},{16,4},{20,0},{24,12},{28,8},{1,21},{... | collective-permute-start | bytes 393224 | tf_op jit(solution)/shard_map/ppermute | solution.py:544
  32.1 3.6 %collective-permute-start.12 = (f32[256,128]{1,0:T(8,128)S(1)}, f32[256,128]{1,0:T(8,128)S(1)}, u32[]{:S(2)}, u32[]{:S(2)}) collective-permute-start(f32[256,128]{1,0:T(8,128)S(1)} %get-tuple-element.57), channel_id=1, source_target_pairs={{0,24},{4,28},{8,16},{12,20},{16,8},{20,12},{24,0},{28,4},{1,25},{... | collective-permute-start | bytes 393224 | tf_op jit(solution)/shard_map/ppermute | solution.py:544
  35.7 1.7 %collective-permute-start.7 = (f32[256,128]{1,0:T(8,128)S(1)}, f32[256,128]{1,0:T(8,128)S(1)}, u32[]{:S(2)}, u32[]{:S(2)}) collective-permute-start(f32[256,128]{1,0:T(8,128)S(1)} %get-tuple-element.52), channel_id=1, source_target_pairs={{0,4},{4,0},{8,12},{12,8},{16,20},{20,16},{24,28},{28,24},{1,5},{5... | collective-permute-start | bytes 393224 | tf_op jit(solution)/shard_map/ppermute | solution.py:544
  37.4 9.0 %collective-permute-done.10.refs_4_ = f32[256,128]{1,0:T(8,128)S(1)} collective-permute-done((f32[256,128]{1,0:T(8,128)S(1)}, f32[256,128]{1,0:T(8,128)S(1)}, u32[]{:S(2)}, u32[]{:S(2)}) %collective-permute-start.10) | collective-permute-done | bytes 131104 | tf_op jit(solution)/shard_map/ppermute | solution.py:544
  46.9 3.6 %collective-permute-done.11.refs_5_ = f32[256,128]{1,0:T(8,128)S(1)} collective-permute-done((f32[256,128]{1,0:T(8,128)S(1)}, f32[256,128]{1,0:T(8,128)S(1)}, u32[]{:S(2)}, u32[]{:S(2)}) %collective-permute-start.11) | collective-permute-done | bytes 131104 | tf_op jit(solution)/shard_map/ppermute | solution.py:544
  51.7 4.6 %collective-permute-done.9.refs_3_ = f32[256,128]{1,0:T(8,128)S(1)} collective-permute-done((f32[256,128]{1,0:T(8,128)S(1)}, f32[256,128]{1,0:T(8,128)S(1)}, u32[]{:S(2)}, u32[]{:S(2)}) %collective-permute-start.9) | collective-permute-done | bytes 131104 | tf_op jit(solution)/shard_map/ppermute | solution.py:544
  56.3 1.4 %shard_map.105 = (f32[256,128]{1,0:T(8,128)S(1)}, f32[256,128]{1,0:T(8,128)S(1)}, f32[256,128]{1,0:T(8,128)S(1)}, f32[256,128]{1,0:T(8,128)S(1)}, f32[128,128]{1...) custom-call(s32[8]{0:T(128)S(1)} %copy-done.1, s32[8]{0:T(128)S(1)} %compare_select_fusion.1.meta, ...), custom_call_target="tpu_custom_call" | custom-call | bytes 1736704 | tf_op jit(solution)/shard_map/pallas_call | solution.py:44
  57.7 2.4 %collective-permute-start.14 = (f32[128,128]{1,0:T(8,128)S(1)}, f32[128,128]{1,0:T(8,128)S(1)}, u32[]{:S(2)}, u32[]{:S(2)}) collective-permute-start(f32[128,128]{1,0:T(8,128)S(1)} %get-tuple-element.60), channel_id=1, source_target_pairs={{0,8},{1,9},{2,10},{3,11},{4,12},{5,13},{6,14},{7,15},{8,16},{9,17... | collective-permute-start | bytes 196616 | tf_op jit(solution)/shard_map/ppermute | solution.py:622
  60.1 2.0 %collective-permute-start.15 = (f32[128,128]{1,0:T(8,128)S(1)}, f32[128,128]{1,0:T(8,128)S(1)}, u32[]{:S(2)}, u32[]{:S(2)}) collective-permute-start(f32[128,128]{1,0:T(8,128)S(1)} %get-tuple-element.60), channel_id=1, source_target_pairs={{0,16},{1,17},{2,18},{3,19},{4,20},{5,21},{6,22},{7,23},{8,24},{9,... | collective-permute-start | bytes 196616 | tf_op jit(solution)/shard_map/ppermute | solution.py:622
  62.1 2.8 %collective-permute-start.16 = (f32[128,128]{1,0:T(8,128)S(1)}, f32[128,128]{1,0:T(8,128)S(1)}, u32[]{:S(2)}, u32[]{:S(2)}) collective-permute-start(f32[128,128]{1,0:T(8,128)S(1)} %get-tuple-element.60), channel_id=1, source_target_pairs={{0,24},{1,25},{2,26},{3,27},{4,28},{5,29},{6,30},{7,31},{8,0},{9,1... | collective-permute-start | bytes 196616 | tf_op jit(solution)/shard_map/ppermute | solution.py:622
  64.9 1.4 %collective-permute-done.15 = f32[128,128]{1,0:T(8,128)S(1)} collective-permute-done((f32[128,128]{1,0:T(8,128)S(1)}, f32[128,128]{1,0:T(8,128)S(1)}, u32[]{:S(2)}, u32[]{:S(2)}) %collective-permute-start.15) | collective-permute-done | bytes 65568 | tf_op jit(solution)/shard_map/ppermute | solution.py:622
  67.1 1.2 collective-permute-start.17
  68.2 3.7 %collective-permute-start.18 = (f32[128,128]{1,0:T(8,128)S(1)}, f32[128,128]{1,0:T(8,128)S(1)}, u32[]{:S(2)}, u32[]{:S(2)}) collective-permute-start(f32[128,128]{1,0:T(8,128)S(1)} %get-tuple-element.66), channel_id=1, source_target_pairs={{0,16},{1,17},{2,18},{3,19},{4,20},{5,21},{6,22},{7,23},{8,24},{9,... | collective-permute-start | bytes 196616 | tf_op jit(solution)/shard_map/ppermute | solution.py:622
  72.0 1.7 %collective-permute-done.17 = f32[128,128]{1,0:T(8,128)S(1)} collective-permute-done((f32[128,128]{1,0:T(8,128)S(1)}, f32[128,128]{1,0:T(8,128)S(1)}, u32[]{:S(2)}, u32[]{:S(2)}) %collective-permute-start.17) | collective-permute-done | bytes 65568 | tf_op jit(solution)/shard_map/ppermute | solution.py:622
  73.7 1.4 %collective-permute-done.18 = f32[128,128]{1,0:T(8,128)S(1)} collective-permute-done((f32[128,128]{1,0:T(8,128)S(1)}, f32[128,128]{1,0:T(8,128)S(1)}, u32[]{:S(2)}, u32[]{:S(2)}) %collective-permute-start.18) | collective-permute-done | bytes 65568 | tf_op jit(solution)/shard_map/ppermute | solution.py:622
  76.4 1.6 %collective-permute-start.21 = (f32[512,128]{1,0:T(8,128)S(1)}, f32[512,128]{1,0:T(8,128)S(1)}, u32[]{:S(2)}, u32[]{:S(2)}) collective-permute-start(f32[512,128]{1,0:T(8,128)S(1)} %pad_maximum_fusion.refs_0_), channel_id=1, source_target_pairs={{0,2},{1,3},{2,0},{3,1},{4,6},{5,7},{6,4},{7,5},{8,10},{9,11},{10,... | collective-permute-start | bytes 786440 | tf_op jit(solution)/shard_map/ppermute | solution.py:629
  80.0 5.6 %collective-permute-done.21.refs_1_ = f32[512,128]{1,0:T(8,128)S(1)} collective-permute-done((f32[512,128]{1,0:T(8,128)S(1)}, f32[512,128]{1,0:T(8,128)S(1)}, u32[]{:S(2)}, u32[]{:S(2)}) %collective-permute-start.21) | collective-permute-done | bytes 262176 | tf_op jit(solution)/shard_map/ppermute | solution.py:629
  85.6 6.3 %collective-permute-done.22.refs_2_ = f32[512,128]{1,0:T(8,128)S(1)} collective-permute-done((f32[512,128]{1,0:T(8,128)S(1)}, f32[512,128]{1,0:T(8,128)S(1)}, u32[]{:S(2)}, u32[]{:S(2)}) %collective-permute-start.22) | collective-permute-done | bytes 262176 | tf_op jit(solution)/shard_map/ppermute | solution.py:629
  94.2 1.7 %collective-permute-start.26 = (f32[1024,128]{1,0:T(8,128)S(1)}, f32[1024,128]{1,0:T(8,128)S(1)}, u32[]{:S(2)}, u32[]{:S(2)}) collective-permute-start(f32[1024,128]{1,0:T(8,128)S(1)} %get-tuple-element.72), channel_id=1, source_target_pairs={{0,6},{1,7},{2,4},{3,5},{4,2},{5,3},{6,0},{7,1},{8,14},{9,15},{10,... | collective-permute-start | bytes 1572872 | tf_op jit(solution)/shard_map/ppermute | solution.py:629
  96.0 25.3 %shard_map.106 = (f32[1440,128]{1,0:T(8,128)S(1)}, bf16[512,512]{1,0:T(8,128)(2,1)S(1)}, bf16[512,512]{1,0:T(8,128)(2,1)S(1)}, bf16[904,512]{1,0:T(8,128)(2,1)S(1)}, bf16[904,512]{1,0:T(8,128)(2,1)S(1)}) custom-call(s32[8]{0:T(128)S(1)} %compare_select_fusion.1.meta, s32[1]{0:T(128)S(6)} %copy.29.front, s32[8]{0:T(128)S(1)} %copy-done.1, ...), custom_call_target="tpu_custom_call" | custom-call | flops 5033164800 | bytes 5750784 | tf_op jit(solution)/shard_map/pallas_call | solution.py:44
  121.4 2.3 %collective-permute-done.26.refs_4_ = f32[1024,128]{1,0:T(8,128)S(1)} collective-permute-done((f32[1024,128]{1,0:T(8,128)S(1)}, f32[1024,128]{1,0:T(8,128)S(1)}, u32[]{:S(2)}, u32[]{:S(2)}) %collective-permute-start.26) | collective-permute-done | bytes 524320 | tf_op jit(solution)/shard_map/ppermute | solution.py:629
  123.7 3.7 %shard_map.107 = (f32[8,128,128]{2,1,0:T(8,128)}, f32[1,128]{1,0:T(1,128)}, f32[2304,128]{1,0:T(8,128)}) custom-call(s32[8]{0:T(128)S(1)} %compare_select_fusion.1.meta, s32[1]{0:T(128)S(6)} %copy.29.front, s32[8]{0:T(128)S(1)} %copy-done.1, f32[32,128]{1,0:T(8,128)S(1)} %get-tuple-element.59.reduced, f32[512,128]{1,0:T(8,128)S(1)} %pad_maximum_fusion.1.refs_0_, ...), custom_call_target="tpu_custom_call" | custom-call | flops 2516582400 | bytes 8110592 | tf_op jit(solution)/shard_map/pallas_call | solution.py:44
  (62 shorter events, 9.2 us)
Async XLA Ops:
  4.7 51.6 %copy-start = (f32[32,128]{1,0:T(8,128)S(1)}, f32[32,128]{1,0:T(8,128)}, u32[]{:S(2)}) copy-start(f32[32,128]{1,0:T(8,128)} %damping.1) | copy-start | bytes 49156
  4.8 4.9 %collective-permute-start = (f32[352,128]{1,0:T(8,128)S(1)}, f32[352,128]{1,0:T(8,128)S(1)}, u32[]{:S(2)}, u32[]{:S(2)}) collective-permute-start(f32[352,128]{1,0:T(8,128)S(1)} %get-tuple-element.44), channel_id=1, source_target_pairs={{0,1},{1,0},{2,3},{3,2},{4,5},{5,4},{6,7},{7,6},{8,9},{9,8},{10,11... | collective-permute-start | bytes 540680 | tf_op jit(solution)/shard_map/ppermute | solution.py:544
  5.3 8.0 %collective-permute-start.1 = (f32[352,128]{1,0:T(8,128)S(1)}, f32[352,128]{1,0:T(8,128)S(1)}, u32[]{:S(2)}, u32[]{:S(2)}) collective-permute-start(f32[352,128]{1,0:T(8,128)S(1)} %get-tuple-element.45), channel_id=1, source_target_pairs={{0,2},{1,3},{2,0},{3,1},{4,6},{5,7},{6,4},{7,5},{8,10},{9,11},{10,... | collective-permute-start | bytes 540680 | tf_op jit(solution)/shard_map/ppermute | solution.py:544
  7.9 8.8 %collective-permute-start.2 = (f32[352,128]{1,0:T(8,128)S(1)}, f32[352,128]{1,0:T(8,128)S(1)}, u32[]{:S(2)}, u32[]{:S(2)}) collective-permute-start(f32[352,128]{1,0:T(8,128)S(1)} %get-tuple-element.46), channel_id=1, source_target_pairs={{0,3},{1,2},{2,1},{3,0},{4,7},{5,6},{6,5},{7,4},{8,11},{9,10},{10,... | collective-permute-start | bytes 540680 | tf_op jit(solution)/shard_map/ppermute | solution.py:544
  7.9 8.8 %collective-permute-start.3 = (f32[352,128]{1,0:T(8,128)S(1)}, f32[352,128]{1,0:T(8,128)S(1)}, u32[]{:S(2)}, u32[]{:S(2)}) collective-permute-start(f32[352,128]{1,0:T(8,128)S(1)} %get-tuple-element.47), channel_id=1, source_target_pairs={{0,4},{1,5},{2,6},{3,7},{4,0},{5,1},{6,2},{7,3},{8,12},{9,13},{10,... | collective-permute-start | bytes 540680 | tf_op jit(solution)/shard_map/ppermute | solution.py:544
  9.7 15.9 %collective-permute-start.4 = (f32[352,128]{1,0:T(8,128)S(1)}, f32[352,128]{1,0:T(8,128)S(1)}, u32[]{:S(2)}, u32[]{:S(2)}) collective-permute-start(f32[352,128]{1,0:T(8,128)S(1)} %get-tuple-element.48), channel_id=1, source_target_pairs={{0,5},{1,4},{2,7},{3,6},{4,1},{5,0},{6,3},{7,2},{8,13},{9,12},{10,... | collective-permute-start | bytes 540680 | tf_op jit(solution)/shard_map/ppermute | solution.py:544
  9.7 15.9 %collective-permute-start.5 = (f32[352,128]{1,0:T(8,128)S(1)}, f32[352,128]{1,0:T(8,128)S(1)}, u32[]{:S(2)}, u32[]{:S(2)}) collective-permute-start(f32[352,128]{1,0:T(8,128)S(1)} %get-tuple-element.49), channel_id=1, source_target_pairs={{0,6},{1,7},{2,4},{3,5},{4,2},{5,3},{6,0},{7,1},{8,14},{9,15},{10,... | collective-permute-start | bytes 540680 | tf_op jit(solution)/shard_map/ppermute | solution.py:544
  13.3 12.3 %collective-permute-start.6 = (f32[352,128]{1,0:T(8,128)S(1)}, f32[352,128]{1,0:T(8,128)S(1)}, u32[]{:S(2)}, u32[]{:S(2)}) collective-permute-start(f32[352,128]{1,0:T(8,128)S(1)} %get-tuple-element.50), channel_id=1, source_target_pairs={{0,7},{1,6},{2,5},{3,4},{4,3},{5,2},{6,1},{7,0},{8,15},{9,14},{10,... | collective-permute-start | bytes 540680 | tf_op jit(solution)/shard_map/ppermute | solution.py:544
  27.8 18.6 %collective-permute-start.10 = (f32[256,128]{1,0:T(8,128)S(1)}, f32[256,128]{1,0:T(8,128)S(1)}, u32[]{:S(2)}, u32[]{:S(2)}) collective-permute-start(f32[256,128]{1,0:T(8,128)S(1)} %get-tuple-element.55), channel_id=1, source_target_pairs={{0,16},{4,20},{8,24},{12,28},{16,0},{20,4},{24,8},{28,12},{1,17},{... | collective-permute-start | bytes 393224 | tf_op jit(solution)/shard_map/ppermute | solution.py:544
  30.8 19.7 %collective-permute-start.11 = (f32[256,128]{1,0:T(8,128)S(1)}, f32[256,128]{1,0:T(8,128)S(1)}, u32[]{:S(2)}, u32[]{:S(2)}) collective-permute-start(f32[256,128]{1,0:T(8,128)S(1)} %get-tuple-element.56), channel_id=1, source_target_pairs={{0,20},{4,16},{8,28},{12,24},{16,4},{20,0},{24,12},{28,8},{1,21},{... | collective-permute-start | bytes 393224 | tf_op jit(solution)/shard_map/ppermute | solution.py:544
  32.1 19.2 %collective-permute-start.12 = (f32[256,128]{1,0:T(8,128)S(1)}, f32[256,128]{1,0:T(8,128)S(1)}, u32[]{:S(2)}, u32[]{:S(2)}) collective-permute-start(f32[256,128]{1,0:T(8,128)S(1)} %get-tuple-element.57), channel_id=1, source_target_pairs={{0,24},{4,28},{8,16},{12,20},{16,8},{20,12},{24,0},{28,4},{1,25},{... | collective-permute-start | bytes 393224 | tf_op jit(solution)/shard_map/ppermute | solution.py:544
  35.7 15.6 %collective-permute-start.13 = (f32[256,128]{1,0:T(8,128)S(1)}, f32[256,128]{1,0:T(8,128)S(1)}, u32[]{:S(2)}, u32[]{:S(2)}) collective-permute-start(f32[256,128]{1,0:T(8,128)S(1)} %get-tuple-element.58), channel_id=1, source_target_pairs={{0,28},{4,24},{8,20},{12,16},{16,12},{20,8},{24,4},{28,0},{1,29},{... | collective-permute-start | bytes 393224 | tf_op jit(solution)/shard_map/ppermute | solution.py:544
  35.7 15.6 %collective-permute-start.7 = (f32[256,128]{1,0:T(8,128)S(1)}, f32[256,128]{1,0:T(8,128)S(1)}, u32[]{:S(2)}, u32[]{:S(2)}) collective-permute-start(f32[256,128]{1,0:T(8,128)S(1)} %get-tuple-element.52), channel_id=1, source_target_pairs={{0,4},{4,0},{8,12},{12,8},{16,20},{20,16},{24,28},{28,24},{1,5},{5... | collective-permute-start | bytes 393224 | tf_op jit(solution)/shard_map/ppermute | solution.py:544
  46.4 5.4 %collective-permute-start.8 = (f32[256,128]{1,0:T(8,128)S(1)}, f32[256,128]{1,0:T(8,128)S(1)}, u32[]{:S(2)}, u32[]{:S(2)}) collective-permute-start(f32[256,128]{1,0:T(8,128)S(1)} %get-tuple-element.53), channel_id=1, source_target_pairs={{0,8},{4,12},{8,0},{12,4},{16,24},{20,28},{24,16},{28,20},{1,9},{5... | collective-permute-start | bytes 393224 | tf_op jit(solution)/shard_map/ppermute | solution.py:544
  50.5 5.9 %collective-permute-start.9 = (f32[256,128]{1,0:T(8,128)S(1)}, f32[256,128]{1,0:T(8,128)S(1)}, u32[]{:S(2)}, u32[]{:S(2)}) collective-permute-start(f32[256,128]{1,0:T(8,128)S(1)} %get-tuple-element.54), channel_id=1, source_target_pairs={{0,12},{4,8},{8,4},{12,0},{16,28},{20,24},{24,20},{28,16},{1,13},{... | collective-permute-start | bytes 393224 | tf_op jit(solution)/shard_map/ppermute | solution.py:544
  57.7 7.2 %collective-permute-start.14 = (f32[128,128]{1,0:T(8,128)S(1)}, f32[128,128]{1,0:T(8,128)S(1)}, u32[]{:S(2)}, u32[]{:S(2)}) collective-permute-start(f32[128,128]{1,0:T(8,128)S(1)} %get-tuple-element.60), channel_id=1, source_target_pairs={{0,8},{1,9},{2,10},{3,11},{4,12},{5,13},{6,14},{7,15},{8,16},{9,17... | collective-permute-start | bytes 196616 | tf_op jit(solution)/shard_map/ppermute | solution.py:622
  60.1 6.2 %collective-permute-start.15 = (f32[128,128]{1,0:T(8,128)S(1)}, f32[128,128]{1,0:T(8,128)S(1)}, u32[]{:S(2)}, u32[]{:S(2)}) collective-permute-start(f32[128,128]{1,0:T(8,128)S(1)} %get-tuple-element.60), channel_id=1, source_target_pairs={{0,16},{1,17},{2,18},{3,19},{4,20},{5,21},{6,22},{7,23},{8,24},{9,... | collective-permute-start | bytes 196616 | tf_op jit(solution)/shard_map/ppermute | solution.py:622
  62.1 5.0 %collective-permute-start.16 = (f32[128,128]{1,0:T(8,128)S(1)}, f32[128,128]{1,0:T(8,128)S(1)}, u32[]{:S(2)}, u32[]{:S(2)}) collective-permute-start(f32[128,128]{1,0:T(8,128)S(1)} %get-tuple-element.60), channel_id=1, source_target_pairs={{0,24},{1,25},{2,26},{3,27},{4,28},{5,29},{6,30},{7,31},{8,0},{9,1... | collective-permute-start | bytes 196616 | tf_op jit(solution)/shard_map/ppermute | solution.py:622
  67.1 6.6 %collective-permute-start.17 = (f32[128,128]{1,0:T(8,128)S(1)}, f32[128,128]{1,0:T(8,128)S(1)}, u32[]{:S(2)}, u32[]{:S(2)}) collective-permute-start(f32[128,128]{1,0:T(8,128)S(1)} %get-tuple-element.66), channel_id=1, source_target_pairs={{0,8},{1,9},{2,10},{3,11},{4,12},{5,13},{6,14},{7,15},{8,16},{9,17... | collective-permute-start | bytes 196616 | tf_op jit(solution)/shard_map/ppermute | solution.py:622
  68.2 6.8 %collective-permute-start.18 = (f32[128,128]{1,0:T(8,128)S(1)}, f32[128,128]{1,0:T(8,128)S(1)}, u32[]{:S(2)}, u32[]{:S(2)}) collective-permute-start(f32[128,128]{1,0:T(8,128)S(1)} %get-tuple-element.66), channel_id=1, source_target_pairs={{0,16},{1,17},{2,18},{3,19},{4,20},{5,21},{6,22},{7,23},{8,24},{9,... | collective-permute-start | bytes 196616 | tf_op jit(solution)/shard_map/ppermute | solution.py:622
  72.0 4.3 %collective-permute-start.19 = (f32[128,128]{1,0:T(8,128)S(1)}, f32[128,128]{1,0:T(8,128)S(1)}, u32[]{:S(2)}, u32[]{:S(2)}) collective-permute-start(f32[128,128]{1,0:T(8,128)S(1)} %get-tuple-element.66), channel_id=1, source_target_pairs={{0,24},{1,25},{2,26},{3,27},{4,28},{5,29},{6,30},{7,31},{8,0},{9,1... | collective-permute-start | bytes 196616 | tf_op jit(solution)/shard_map/ppermute | solution.py:622
  76.3 3.6 %collective-permute-start.20 = (f32[1024,128]{1,0:T(8,128)S(1)}, f32[1024,128]{1,0:T(8,128)S(1)}, u32[]{:S(2)}, u32[]{:S(2)}) collective-permute-start(f32[1024,128]{1,0:T(8,128)S(1)} %constant_dynamic-update-slice_fusion), channel_id=1, source_target_pairs={{0,1},{1,0},{2,3},{3,2},{4,5},{5,4},{6,7},{7,6},{8,9},{9,8},{10,11... | collective-permute-start | bytes 1572872 | tf_op jit(solution)/shard_map/ppermute | solution.py:637
  76.4 9.2 %collective-permute-start.21 = (f32[512,128]{1,0:T(8,128)S(1)}, f32[512,128]{1,0:T(8,128)S(1)}, u32[]{:S(2)}, u32[]{:S(2)}) collective-permute-start(f32[512,128]{1,0:T(8,128)S(1)} %pad_maximum_fusion.refs_0_), channel_id=1, source_target_pairs={{0,2},{1,3},{2,0},{3,1},{4,6},{5,7},{6,4},{7,5},{8,10},{9,11},{10,... | collective-permute-start | bytes 786440 | tf_op jit(solution)/shard_map/ppermute | solution.py:629
  78.0 14.0 %collective-permute-start.22 = (f32[512,128]{1,0:T(8,128)S(1)}, f32[512,128]{1,0:T(8,128)S(1)}, u32[]{:S(2)}, u32[]{:S(2)}) collective-permute-start(f32[512,128]{1,0:T(8,128)S(1)} %pad_maximum_fusion.refs_0_), channel_id=1, source_target_pairs={{0,4},{1,5},{2,6},{3,7},{4,0},{5,1},{6,2},{7,3},{8,12},{9,13},{10,... | collective-permute-start | bytes 786440 | tf_op jit(solution)/shard_map/ppermute | solution.py:629
  79.1 12.9 %collective-permute-start.23 = (f32[512,128]{1,0:T(8,128)S(1)}, f32[512,128]{1,0:T(8,128)S(1)}, u32[]{:S(2)}, u32[]{:S(2)}) collective-permute-start(f32[512,128]{1,0:T(8,128)S(1)} %pad_maximum_fusion.refs_0_), channel_id=1, source_target_pairs={{0,6},{1,7},{2,4},{3,5},{4,2},{5,3},{6,0},{7,1},{8,14},{9,15},{10,... | collective-permute-start | bytes 786440 | tf_op jit(solution)/shard_map/ppermute | solution.py:629
  80.0 13.3 %collective-permute-start.27 = (f32[512,128]{1,0:T(8,128)S(1)}, f32[512,128]{1,0:T(8,128)S(1)}, u32[]{:S(2)}, u32[]{:S(2)}) collective-permute-start(f32[512,128]{1,0:T(8,128)S(1)} %pad_maximum_fusion.refs_0_), channel_id=1, source_target_pairs={{0,1},{1,0},{2,3},{3,2},{4,5},{5,4},{6,7},{7,6},{8,9},{9,8},{10,11... | collective-permute-start | bytes 786440 | tf_op jit(solution)/shard_map/ppermute | solution.py:635
  92.0 2.3 %collective-permute-start.28 = (f32[512,128]{1,0:T(8,128)S(1)}, f32[512,128]{1,0:T(8,128)S(1)}, u32[]{:S(2)}, u32[]{:S(2)}) collective-permute-start(f32[512,128]{1,0:T(8,128)S(1)} %collective-permute-done.21.refs_1_), channel_id=1, source_target_pairs={{0,1},{1,0},{2,3},{3,2},{4,5},{5,4},{6,7},{7,6},{8,9},{9,8},{10,11... | collective-permute-start | bytes 786440 | tf_op jit(solution)/shard_map/ppermute | solution.py:643
  92.0 31.7 %collective-permute-start.24 = (f32[1536,128]{1,0:T(8,128)S(1)}, f32[1536,128]{1,0:T(8,128)S(1)}, u32[]{:S(2)}, u32[]{:S(2)}) collective-permute-start(f32[1536,128]{1,0:T(8,128)S(1)} %slice_dynamic-update-slice_fusion.2), channel_id=1, source_target_pairs={{0,2},{1,3},{2,0},{3,1},{4,6},{5,7},{6,4},{7,5},{8,10},{9,11},{10,... | collective-permute-start | bytes 2359304 | tf_op jit(solution)/shard_map/ppermute | solution.py:629
  92.8 3.2 %collective-permute-start.29 = (f32[512,128]{1,0:T(8,128)S(1)}, f32[512,128]{1,0:T(8,128)S(1)}, u32[]{:S(2)}, u32[]{:S(2)}) collective-permute-start(f32[512,128]{1,0:T(8,128)S(1)} %collective-permute-done.22.refs_2_), channel_id=1, source_target_pairs={{0,1},{1,0},{2,3},{3,2},{4,5},{5,4},{6,7},{7,6},{8,9},{9,8},{10,11... | collective-permute-start | bytes 786440 | tf_op jit(solution)/shard_map/ppermute | solution.py:643
  93.0 3.0 %collective-permute-start.30 = (f32[512,128]{1,0:T(8,128)S(1)}, f32[512,128]{1,0:T(8,128)S(1)}, u32[]{:S(2)}, u32[]{:S(2)}) collective-permute-start(f32[512,128]{1,0:T(8,128)S(1)} %collective-permute-done.23.refs_3_), channel_id=1, source_target_pairs={{0,1},{1,0},{2,3},{3,2},{4,5},{5,4},{6,7},{7,6},{8,9},{9,8},{10,11... | collective-permute-start | bytes 786440 | tf_op jit(solution)/shard_map/ppermute | solution.py:643
  93.3 28.1 %collective-permute-start.25 = (f32[1024,128]{1,0:T(8,128)S(1)}, f32[1024,128]{1,0:T(8,128)S(1)}, u32[]{:S(2)}, u32[]{:S(2)}) collective-permute-start(f32[1024,128]{1,0:T(8,128)S(1)} %get-tuple-element.72), channel_id=1, source_target_pairs={{0,4},{1,5},{2,6},{3,7},{4,0},{5,1},{6,2},{7,3},{8,12},{9,13},{10,... | collective-permute-start | bytes 1572872 | tf_op jit(solution)/shard_map/ppermute | solution.py:629
  94.2 29.5 %collective-permute-start.26 = (f32[1024,128]{1,0:T(8,128)S(1)}, f32[1024,128]{1,0:T(8,128)S(1)}, u32[]{:S(2)}, u32[]{:S(2)}) collective-permute-start(f32[1024,128]{1,0:T(8,128)S(1)} %get-tuple-element.72), channel_id=1, source_target_pairs={{0,6},{1,7},{2,4},{3,5},{4,2},{5,3},{6,0},{7,1},{8,14},{9,15},{10,... | collective-permute-start | bytes 1572872 | tf_op jit(solution)/shard_map/ppermute | solution.py:629
  (5 other events, 29.3 us)

commit v2 on v1

--- a/solution.py
+++ b/solution.py
@@ -182,8 +182,9 @@
     rhs[...] = jnp.zeros_like(rhs)
     for j in range(GROUP):
         rhs[j : j + BAND, :] = rhs[j : j + BAND, :] + got[j, PAIRS * piece : PAIRS * piece + BAND, :]
+    share = pl.ds(pl.multiple_of(place // (GROUP // 2) * BAND, BAND), BAND)
     for dest in range(pts_count):
-        out[dest, capacity * piece : capacity * piece + 2 * BAND, :] = rhs[...]
+        out[dest, capacity * piece : capacity * piece + BAND, :] = rhs[share, :]
     for bit in range(sends):
         outs[bit][...] = out[bit] if sends > 1 else out[...]
 
@@ -253,7 +254,7 @@
         before = (plane + planes - 1) % planes
         reduced[plane * GROUP : (plane + 1) * GROUP, :] = (
             got[plane * members, tail : tail + BAND, :]
-            + got[before * members, tail + BAND : tail + 2 * BAND, :]
+            + got[before * members + 1, tail : tail + BAND, :]
         )
 
 
@@ -572,7 +573,7 @@
     )
     got = flip(sent, AXES, clusters)
     sends = pts_count if pts_count <= GROUP else 1
-    send_rows = capacity * piece + 2 * BAND
+    send_rows = capacity * piece + BAND
     shape = (send_rows, rows) if sends > 1 else (pts_count, send_rows, rows)
     sent = call(
         functools.partial(merge_kernel, (piece, pts_count, capacity, sends)),
@@ -639,7 +640,7 @@
     chunk = BAND * quarter
     both = jnp.concatenate([mirror, swapped[:count]])
     more = jnp.concatenate([both, chunks[2], swapped[count + chunk :]])
-    both, more, *mine = lax.optimization_barrier((both, more, *mine))
+    both, more, mine[-1] = lax.optimization_barrier((both, more, mine[-1]))
     theirs += [lax.ppermute(x, AXES, swap) for x in mine[1:]]
     sides = [mirror, swapped, *across([more, both, both]), chunks[0]]
 

time: 128 us -> 125 us (0.977)
  waiting for transfers between devices: 49.9 us -> 46.8 us
    ppermute x6, waiting for transfers between devices: 14.3 us -> 11.8 us  [across(): moved.append(lax.ppermute(value, AXES, pairs))]
where the time goes in v2:
time: 125 us
  waiting for transfers between devices  46.8 us (37%)
  starting transfers between devices  39.7 us (32%)
  Pallas kernels  35.2 us (28%)
  local copies, waits for them, and re-layouts  1.58 us (1%)
  between operations  1.57 us (1%)
    pallas_call x5, Pallas kernels, call(): pl.pallas_call(kernel, out_shape=out_shapes, in_specs=[spec(s) for s in s...  35.2 us
    ppermute x14, waiting for transfers between devices, flip(): lax.ppermute(value, axis, [(p, p ^ bit + 1) for p in range(count)])  28.7 us
    ppermute x14, starting transfers between devices, flip(): lax.ppermute(value, axis, [(p, p ^ bit + 1) for p in range(count)])  19.4 us
    ppermute x6, starting transfers between devices, along(): moved.append(lax.ppermute(value, AXES, pairs))  12 us
    ppermute x6, waiting for transfers between devices, across(): moved.append(lax.ppermute(value, AXES, pairs))  11.8 us
    ppermute x6, starting transfers between devices, across(): moved.append(lax.ppermute(value, AXES, pairs))  7.75 us
    ppermute x6, waiting for transfers between devices, along(): moved.append(lax.ppermute(value, AXES, pairs))  6.3 us
  transfers between devices with their start and end apart: 31, of which 15 were waited for; matrix products, arithmetic and copies ran while one was open for 0% of the time, Pallas kernels for 20%

profile of v2, /device:TPU:0, one launch (start us, length us, event | category | flops | bytes accessed | tf_op | source)
XLA Modules:
  0.0 124.9 jit_solution(17149713459338844221)
XLA Ops:
  0.7 1.4 %copy.15 = bf16[1,6,128,3,256]{4,2,1,3,0:T(8,128)(2,1)S(1)} copy(bf16[1,6,128,3,256]{4,2,3,1,0:T(8,128)(2,1)} %param.8) | data formatting | bytes 2359296 | tf_op args[0]
  2.1 2.6 %shard_map.103 = (f32[352,128]{1,0:T(8,128)S(1)}, f32[352,128]{1,0:T(8,128)S(1)}, f32[352,128]{1,0:T(8,128)S(1)}, f32[352,128]{1,0:T(8,128)S(1)}, f32[352,128]{1...) custom-call(s32[8]{0:T(128)S(1)} %compare_select_fusion.1.meta, ...), custom_call_target="tpu_custom_call" | custom-call | flops 528482304 | bytes 2629632 | tf_op jit(solution)/shard_map/pallas_call | solution.py:44
  5.3 2.6 %collective-permute-start.1 = (f32[352,128]{1,0:T(8,128)S(1)}, f32[352,128]{1,0:T(8,128)S(1)}, u32[]{:S(2)}, u32[]{:S(2)}) collective-permute-start(f32[352,128]{1,0:T(8,128)S(1)} %get-tuple-element.42), channel_id=1, source_target_pairs={{0,2},{1,3},{2,0},{3,1},{4,6},{5,7},{6,4},{7,5},{8,10},{9,11},{10,... | collective-permute-start | bytes 540680 | tf_op jit(solution)/shard_map/ppermute | solution.py:545
  7.9 1.8 %collective-permute-start.3 = (f32[352,128]{1,0:T(8,128)S(1)}, f32[352,128]{1,0:T(8,128)S(1)}, u32[]{:S(2)}, u32[]{:S(2)}) collective-permute-start(f32[352,128]{1,0:T(8,128)S(1)} %get-tuple-element.44), channel_id=1, source_target_pairs={{0,4},{1,5},{2,6},{3,7},{4,0},{5,1},{6,2},{7,3},{8,12},{9,13},{10,... | collective-permute-start | bytes 540680 | tf_op jit(solution)/shard_map/ppermute | solution.py:545
  9.7 2.6 %collective-permute-start.5 = (f32[352,128]{1,0:T(8,128)S(1)}, f32[352,128]{1,0:T(8,128)S(1)}, u32[]{:S(2)}, u32[]{:S(2)}) collective-permute-start(f32[352,128]{1,0:T(8,128)S(1)} %get-tuple-element.46), channel_id=1, source_target_pairs={{0,6},{1,7},{2,4},{3,5},{4,2},{5,3},{6,0},{7,1},{8,14},{9,15},{10,... | collective-permute-start | bytes 540680 | tf_op jit(solution)/shard_map/ppermute | solution.py:545
  13.3 1.6 %collective-permute-start.6 = (f32[352,128]{1,0:T(8,128)S(1)}, f32[352,128]{1,0:T(8,128)S(1)}, u32[]{:S(2)}, u32[]{:S(2)}) collective-permute-start(f32[352,128]{1,0:T(8,128)S(1)} %get-tuple-element.47), channel_id=1, source_target_pairs={{0,7},{1,6},{2,5},{3,4},{4,3},{5,2},{6,1},{7,0},{8,15},{9,14},{10,... | collective-permute-start | bytes 540680 | tf_op jit(solution)/shard_map/ppermute | solution.py:545
  14.9 1.8 %collective-permute-done.2.refs_3_ = f32[352,128]{1,0:T(8,128)S(1)} collective-permute-done((f32[352,128]{1,0:T(8,128)S(1)}, f32[352,128]{1,0:T(8,128)S(1)}, u32[]{:S(2)}, u32[]{:S(2)}) %collective-permute-start.2) | collective-permute-done | bytes 180256 | tf_op jit(solution)/shard_map/ppermute | solution.py:545
  16.7 8.9 %collective-permute-done.4.refs_5_ = f32[352,128]{1,0:T(8,128)S(1)} collective-permute-done((f32[352,128]{1,0:T(8,128)S(1)}, f32[352,128]{1,0:T(8,128)S(1)}, u32[]{:S(2)}, u32[]{:S(2)}) %collective-permute-start.4) | collective-permute-done | bytes 180256 | tf_op jit(solution)/shard_map/ppermute | solution.py:545
  25.6 2.2 %shard_map.104 = (f32[248,128]{1,0:T(8,128)S(1)}, f32[248,128]{1,0:T(8,128)S(1)}, f32[248,128]{1,0:T(8,128)S(1)}, f32[248,128]{1,0:T(8,128)S(1)}, f32[248,128]{1...) custom-call(s32[8]{0:T(128)S(1)} %copy-done.1, ...), custom_call_target="tpu_custom_call" | custom-call | bytes 2457600 | tf_op jit(solution)/shard_map/pallas_call | solution.py:44
  27.8 3.0 %collective-permute-start.10 = (f32[248,128]{1,0:T(8,128)S(1)}, f32[248,128]{1,0:T(8,128)S(1)}, u32[]{:S(2)}, u32[]{:S(2)}) collective-permute-start(f32[248,128]{1,0:T(8,128)S(1)} %get-tuple-element.52), channel_id=1, source_target_pairs={{0,16},{4,20},{8,24},{12,28},{16,0},{20,4},{24,8},{28,12},{1,17},{... | collective-permute-start | bytes 380936 | tf_op jit(solution)/shard_map/ppermute | solution.py:545
  30.8 1.3 %collective-permute-start.11 = (f32[248,128]{1,0:T(8,128)S(1)}, f32[248,128]{1,0:T(8,128)S(1)}, u32[]{:S(2)}, u32[]{:S(2)}) collective-permute-start(f32[248,128]{1,0:T(8,128)S(1)} %get-tuple-element.53), channel_id=1, source_target_pairs={{0,20},{4,16},{8,28},{12,24},{16,4},{20,0},{24,12},{28,8},{1,21},{... | collective-permute-start | bytes 380936 | tf_op jit(solution)/shard_map/ppermute | solution.py:545
  32.1 3.6 %collective-permute-start.12 = (f32[248,128]{1,0:T(8,128)S(1)}, f32[248,128]{1,0:T(8,128)S(1)}, u32[]{:S(2)}, u32[]{:S(2)}) collective-permute-start(f32[248,128]{1,0:T(8,128)S(1)} %get-tuple-element.54), channel_id=1, source_target_pairs={{0,24},{4,28},{8,16},{12,20},{16,8},{20,12},{24,0},{28,4},{1,25},{... | collective-permute-start | bytes 380936 | tf_op jit(solution)/shard_map/ppermute | solution.py:545
  35.7 1.7 %collective-permute-start.7 = (f32[248,128]{1,0:T(8,128)S(1)}, f32[248,128]{1,0:T(8,128)S(1)}, u32[]{:S(2)}, u32[]{:S(2)}) collective-permute-start(f32[248,128]{1,0:T(8,128)S(1)} %get-tuple-element.49), channel_id=1, source_target_pairs={{0,4},{4,0},{8,12},{12,8},{16,20},{20,16},{24,28},{28,24},{1,5},{5... | collective-permute-start | bytes 380936 | tf_op jit(solution)/shard_map/ppermute | solution.py:545
  37.4 8.6 %collective-permute-done.10.refs_4_ = f32[248,128]{1,0:T(8,128)S(1)} collective-permute-done((f32[248,128]{1,0:T(8,128)S(1)}, f32[248,128]{1,0:T(8,128)S(1)}, u32[]{:S(2)}, u32[]{:S(2)}) %collective-permute-start.10) | collective-permute-done | bytes 127008 | tf_op jit(solution)/shard_map/ppermute | solution.py:545
  46.4 3.5 %collective-permute-done.11.refs_5_ = f32[248,128]{1,0:T(8,128)S(1)} collective-permute-done((f32[248,128]{1,0:T(8,128)S(1)}, f32[248,128]{1,0:T(8,128)S(1)}, u32[]{:S(2)}, u32[]{:S(2)}) %collective-permute-start.11) | collective-permute-done | bytes 127008 | tf_op jit(solution)/shard_map/ppermute | solution.py:545
  51.1 4.7 %collective-permute-done.9.refs_3_ = f32[248,128]{1,0:T(8,128)S(1)} collective-permute-done((f32[248,128]{1,0:T(8,128)S(1)}, f32[248,128]{1,0:T(8,128)S(1)}, u32[]{:S(2)}, u32[]{:S(2)}) %collective-permute-start.9) | collective-permute-done | bytes 127008 | tf_op jit(solution)/shard_map/ppermute | solution.py:545
  55.8 1.4 %shard_map.105 = (f32[256,128]{1,0:T(8,128)S(1)}, f32[256,128]{1,0:T(8,128)S(1)}, f32[256,128]{1,0:T(8,128)S(1)}, f32[256,128]{1,0:T(8,128)S(1)}, f32[128,128]{1...) custom-call(s32[8]{0:T(128)S(1)} %copy-done.1, s32[8]{0:T(128)S(1)} %compare_select_fusion.1.meta, ...), custom_call_target="tpu_custom_call" | custom-call | bytes 1703936 | tf_op jit(solution)/shard_map/pallas_call | solution.py:44
  57.1 2.1 %collective-permute-start.14 = (f32[128,128]{1,0:T(8,128)S(1)}, f32[128,128]{1,0:T(8,128)S(1)}, u32[]{:S(2)}, u32[]{:S(2)}) collective-permute-start(f32[128,128]{1,0:T(8,128)S(1)} %get-tuple-element.57), channel_id=1, source_target_pairs={{0,8},{1,9},{2,10},{3,11},{4,12},{5,13},{6,14},{7,15},{8,16},{9,17... | collective-permute-start | bytes 196616 | tf_op jit(solution)/shard_map/ppermute | solution.py:623
  59.3 2.1 %collective-permute-start.15 = (f32[128,128]{1,0:T(8,128)S(1)}, f32[128,128]{1,0:T(8,128)S(1)}, u32[]{:S(2)}, u32[]{:S(2)}) collective-permute-start(f32[128,128]{1,0:T(8,128)S(1)} %get-tuple-element.57), channel_id=1, source_target_pairs={{0,16},{1,17},{2,18},{3,19},{4,20},{5,21},{6,22},{7,23},{8,24},{9,... | collective-permute-start | bytes 196616 | tf_op jit(solution)/shard_map/ppermute | solution.py:623
  61.4 2.8 %collective-permute-start.16 = (f32[128,128]{1,0:T(8,128)S(1)}, f32[128,128]{1,0:T(8,128)S(1)}, u32[]{:S(2)}, u32[]{:S(2)}) collective-permute-start(f32[128,128]{1,0:T(8,128)S(1)} %get-tuple-element.57), channel_id=1, source_target_pairs={{0,24},{1,25},{2,26},{3,27},{4,28},{5,29},{6,30},{7,31},{8,0},{9,1... | collective-permute-start | bytes 196616 | tf_op jit(solution)/shard_map/ppermute | solution.py:623
  64.2 1.4 %collective-permute-done.15 = f32[128,128]{1,0:T(8,128)S(1)} collective-permute-done((f32[128,128]{1,0:T(8,128)S(1)}, f32[128,128]{1,0:T(8,128)S(1)}, u32[]{:S(2)}, u32[]{:S(2)}) %collective-permute-start.15) | collective-permute-done | bytes 65568 | tf_op jit(solution)/shard_map/ppermute | solution.py:623
  66.3 1.2 collective-permute-start.17
  67.5 3.7 %collective-permute-start.18 = (f32[128,128]{1,0:T(8,128)S(1)}, f32[128,128]{1,0:T(8,128)S(1)}, u32[]{:S(2)}, u32[]{:S(2)}) collective-permute-start(f32[128,128]{1,0:T(8,128)S(1)} %get-tuple-element.63), channel_id=1, source_target_pairs={{0,16},{1,17},{2,18},{3,19},{4,20},{5,21},{6,22},{7,23},{8,24},{9,... | collective-permute-start | bytes 196616 | tf_op jit(solution)/shard_map/ppermute | solution.py:623
  71.2 1.7 %collective-permute-done.17 = f32[128,128]{1,0:T(8,128)S(1)} collective-permute-done((f32[128,128]{1,0:T(8,128)S(1)}, f32[128,128]{1,0:T(8,128)S(1)}, u32[]{:S(2)}, u32[]{:S(2)}) %collective-permute-start.17) | collective-permute-done | bytes 65568 | tf_op jit(solution)/shard_map/ppermute | solution.py:623
  72.9 1.4 %collective-permute-done.18 = f32[128,128]{1,0:T(8,128)S(1)} collective-permute-done((f32[128,128]{1,0:T(8,128)S(1)}, f32[128,128]{1,0:T(8,128)S(1)}, u32[]{:S(2)}, u32[]{:S(2)}) %collective-permute-start.18) | collective-permute-done | bytes 65568 | tf_op jit(solution)/shard_map/ppermute | solution.py:623
  75.7 1.6 %collective-permute-start.25 = (f32[512,128]{1,0:T(8,128)S(1)}, f32[512,128]{1,0:T(8,128)S(1)}, u32[]{:S(2)}, u32[]{:S(2)}) collective-permute-start(f32[512,128]{1,0:T(8,128)S(1)} %pad_maximum_fusion.refs_0_), channel_id=1, source_target_pairs={{0,2},{1,3},{2,0},{3,1},{4,6},{5,7},{6,4},{7,5},{8,10},{9,11},{10,... | collective-permute-start | bytes 786440 | tf_op jit(solution)/shard_map/ppermute | solution.py:630
  79.2 5.7 %collective-permute-done.25.refs_1_ = f32[512,128]{1,0:T(8,128)S(1)} collective-permute-done((f32[512,128]{1,0:T(8,128)S(1)}, f32[512,128]{1,0:T(8,128)S(1)}, u32[]{:S(2)}, u32[]{:S(2)}) %collective-permute-start.25) | collective-permute-done | bytes 262176 | tf_op jit(solution)/shard_map/ppermute | solution.py:630
  85.0 5.7 %collective-permute-done.21.refs_3_ = f32[512,128]{1,0:T(8,128)S(1)} collective-permute-done((f32[512,128]{1,0:T(8,128)S(1)}, f32[512,128]{1,0:T(8,128)S(1)}, u32[]{:S(2)}, u32[]{:S(2)}) %collective-permute-start.21) | collective-permute-done | bytes 262176 | tf_op jit(solution)/shard_map/ppermute | solution.py:630
  90.7 1.4 %collective-permute-start.22 = (f32[1536,128]{1,0:T(8,128)S(1)}, f32[1536,128]{1,0:T(8,128)S(1)}, u32[]{:S(2)}, u32[]{:S(2)}) collective-permute-start(f32[1536,128]{1,0:T(8,128)S(1)} %slice_dynamic-update-slice_fusion.2), channel_id=1, source_target_pairs={{0,2},{1,3},{2,0},{3,1},{4,6},{5,7},{6,4},{7,5},{8,10},{9,11},{10,... | collective-permute-start | bytes 2359304 | tf_op jit(solution)/shard_map/ppermute | solution.py:630
  93.5 1.9 %collective-permute-start.24 = (f32[1024,128]{1,0:T(8,128)S(1)}, f32[1024,128]{1,0:T(8,128)S(1)}, u32[]{:S(2)}, u32[]{:S(2)}) collective-permute-start(f32[1024,128]{1,0:T(8,128)S(1)} %get-tuple-element.69), channel_id=1, source_target_pairs={{0,6},{1,7},{2,4},{3,5},{4,2},{5,3},{6,0},{7,1},{8,14},{9,15},{10,... | collective-permute-start | bytes 1572872 | tf_op jit(solution)/shard_map/ppermute | solution.py:630
  95.5 25.3 %shard_map.106 = (f32[1440,128]{1,0:T(8,128)S(1)}, bf16[512,512]{1,0:T(8,128)(2,1)S(1)}, bf16[512,512]{1,0:T(8,128)(2,1)S(1)}, bf16[904,512]{1,0:T(8,128)(2,1)S(1)}, bf16[904,512]{1,0:T(8,128)(2,1)S(1)}) custom-call(s32[8]{0:T(128)S(1)} %compare_select_fusion.1.meta, s32[1]{0:T(128)S(6)} %copy.29.front, s32[8]{0:T(128)S(1)} %copy-done.1, ...), custom_call_target="tpu_custom_call" | custom-call | flops 5033164800 | bytes 5750784 | tf_op jit(solution)/shard_map/pallas_call | solution.py:44
  121.2 3.7 %shard_map.107 = (f32[8,128,128]{2,1,0:T(8,128)}, f32[1,128]{1,0:T(1,128)}, f32[2304,128]{1,0:T(8,128)}) custom-call(s32[8]{0:T(128)S(1)} %compare_select_fusion.1.meta, s32[1]{0:T(128)S(6)} %copy.29.front, s32[8]{0:T(128)S(1)} %copy-done.1, f32[32,128]{1,0:T(8,128)S(1)} %get-tuple-element.56.reduced, f32[512,128]{1,0:T(8,128)S(1)} %pad_maximum_fusion.1.refs_0_, ...), custom_call_target="tpu_custom_call" | custom-call | flops 2516582400 | bytes 8110592 | tf_op jit(solution)/shard_map/pallas_call | solution.py:44
  (62 shorter events, 8.5 us)
Async XLA Ops:
  4.7 51.0 %copy-start = (f32[32,128]{1,0:T(8,128)S(1)}, f32[32,128]{1,0:T(8,128)}, u32[]{:S(2)}) copy-start(f32[32,128]{1,0:T(8,128)} %damping.1) | copy-start | bytes 49156
  4.8 4.9 %collective-permute-start = (f32[352,128]{1,0:T(8,128)S(1)}, f32[352,128]{1,0:T(8,128)S(1)}, u32[]{:S(2)}, u32[]{:S(2)}) collective-permute-start(f32[352,128]{1,0:T(8,128)S(1)} %get-tuple-element.41), channel_id=1, source_target_pairs={{0,1},{1,0},{2,3},{3,2},{4,5},{5,4},{6,7},{7,6},{8,9},{9,8},{10,11... | collective-permute-start | bytes 540680 | tf_op jit(solution)/shard_map/ppermute | solution.py:545
  5.3 8.0 %collective-permute-start.1 = (f32[352,128]{1,0:T(8,128)S(1)}, f32[352,128]{1,0:T(8,128)S(1)}, u32[]{:S(2)}, u32[]{:S(2)}) collective-permute-start(f32[352,128]{1,0:T(8,128)S(1)} %get-tuple-element.42), channel_id=1, source_target_pairs={{0,2},{1,3},{2,0},{3,1},{4,6},{5,7},{6,4},{7,5},{8,10},{9,11},{10,... | collective-permute-start | bytes 540680 | tf_op jit(solution)/shard_map/ppermute | solution.py:545
  7.9 8.8 %collective-permute-start.2 = (f32[352,128]{1,0:T(8,128)S(1)}, f32[352,128]{1,0:T(8,128)S(1)}, u32[]{:S(2)}, u32[]{:S(2)}) collective-permute-start(f32[352,128]{1,0:T(8,128)S(1)} %get-tuple-element.43), channel_id=1, source_target_pairs={{0,3},{1,2},{2,1},{3,0},{4,7},{5,6},{6,5},{7,4},{8,11},{9,10},{10,... | collective-permute-start | bytes 540680 | tf_op jit(solution)/shard_map/ppermute | solution.py:545
  7.9 8.8 %collective-permute-start.3 = (f32[352,128]{1,0:T(8,128)S(1)}, f32[352,128]{1,0:T(8,128)S(1)}, u32[]{:S(2)}, u32[]{:S(2)}) collective-permute-start(f32[352,128]{1,0:T(8,128)S(1)} %get-tuple-element.44), channel_id=1, source_target_pairs={{0,4},{1,5},{2,6},{3,7},{4,0},{5,1},{6,2},{7,3},{8,12},{9,13},{10,... | collective-permute-start | bytes 540680 | tf_op jit(solution)/shard_map/ppermute | solution.py:545
  9.7 15.9 %collective-permute-start.4 = (f32[352,128]{1,0:T(8,128)S(1)}, f32[352,128]{1,0:T(8,128)S(1)}, u32[]{:S(2)}, u32[]{:S(2)}) collective-permute-start(f32[352,128]{1,0:T(8,128)S(1)} %get-tuple-element.45), channel_id=1, source_target_pairs={{0,5},{1,4},{2,7},{3,6},{4,1},{5,0},{6,3},{7,2},{8,13},{9,12},{10,... | collective-permute-start | bytes 540680 | tf_op jit(solution)/shard_map/ppermute | solution.py:545
  9.7 15.9 %collective-permute-start.5 = (f32[352,128]{1,0:T(8,128)S(1)}, f32[352,128]{1,0:T(8,128)S(1)}, u32[]{:S(2)}, u32[]{:S(2)}) collective-permute-start(f32[352,128]{1,0:T(8,128)S(1)} %get-tuple-element.46), channel_id=1, source_target_pairs={{0,6},{1,7},{2,4},{3,5},{4,2},{5,3},{6,0},{7,1},{8,14},{9,15},{10,... | collective-permute-start | bytes 540680 | tf_op jit(solution)/shard_map/ppermute | solution.py:545
  13.3 12.3 %collective-permute-start.6 = (f32[352,128]{1,0:T(8,128)S(1)}, f32[352,128]{1,0:T(8,128)S(1)}, u32[]{:S(2)}, u32[]{:S(2)}) collective-permute-start(f32[352,128]{1,0:T(8,128)S(1)} %get-tuple-element.47), channel_id=1, source_target_pairs={{0,7},{1,6},{2,5},{3,4},{4,3},{5,2},{6,1},{7,0},{8,15},{9,14},{10,... | collective-permute-start | bytes 540680 | tf_op jit(solution)/shard_map/ppermute | solution.py:545
  27.8 18.1 %collective-permute-start.10 = (f32[248,128]{1,0:T(8,128)S(1)}, f32[248,128]{1,0:T(8,128)S(1)}, u32[]{:S(2)}, u32[]{:S(2)}) collective-permute-start(f32[248,128]{1,0:T(8,128)S(1)} %get-tuple-element.52), channel_id=1, source_target_pairs={{0,16},{4,20},{8,24},{12,28},{16,0},{20,4},{24,8},{28,12},{1,17},{... | collective-permute-start | bytes 380936 | tf_op jit(solution)/shard_map/ppermute | solution.py:545
  30.8 19.2 %collective-permute-start.11 = (f32[248,128]{1,0:T(8,128)S(1)}, f32[248,128]{1,0:T(8,128)S(1)}, u32[]{:S(2)}, u32[]{:S(2)}) collective-permute-start(f32[248,128]{1,0:T(8,128)S(1)} %get-tuple-element.53), channel_id=1, source_target_pairs={{0,20},{4,16},{8,28},{12,24},{16,4},{20,0},{24,12},{28,8},{1,21},{... | collective-permute-start | bytes 380936 | tf_op jit(solution)/shard_map/ppermute | solution.py:545
  32.1 18.7 %collective-permute-start.12 = (f32[248,128]{1,0:T(8,128)S(1)}, f32[248,128]{1,0:T(8,128)S(1)}, u32[]{:S(2)}, u32[]{:S(2)}) collective-permute-start(f32[248,128]{1,0:T(8,128)S(1)} %get-tuple-element.54), channel_id=1, source_target_pairs={{0,24},{4,28},{8,16},{12,20},{16,8},{20,12},{24,0},{28,4},{1,25},{... | collective-permute-start | bytes 380936 | tf_op jit(solution)/shard_map/ppermute | solution.py:545
  35.7 15.1 %collective-permute-start.13 = (f32[248,128]{1,0:T(8,128)S(1)}, f32[248,128]{1,0:T(8,128)S(1)}, u32[]{:S(2)}, u32[]{:S(2)}) collective-permute-start(f32[248,128]{1,0:T(8,128)S(1)} %get-tuple-element.55), channel_id=1, source_target_pairs={{0,28},{4,24},{8,20},{12,16},{16,12},{20,8},{24,4},{28,0},{1,29},{... | collective-permute-start | bytes 380936 | tf_op jit(solution)/shard_map/ppermute | solution.py:545
  35.7 15.1 %collective-permute-start.7 = (f32[248,128]{1,0:T(8,128)S(1)}, f32[248,128]{1,0:T(8,128)S(1)}, u32[]{:S(2)}, u32[]{:S(2)}) collective-permute-start(f32[248,128]{1,0:T(8,128)S(1)} %get-tuple-element.49), channel_id=1, source_target_pairs={{0,4},{4,0},{8,12},{12,8},{16,20},{20,16},{24,28},{28,24},{1,5},{5... | collective-permute-start | bytes 380936 | tf_op jit(solution)/shard_map/ppermute | solution.py:545
  45.9 5.2 %collective-permute-start.8 = (f32[248,128]{1,0:T(8,128)S(1)}, f32[248,128]{1,0:T(8,128)S(1)}, u32[]{:S(2)}, u32[]{:S(2)}) collective-permute-start(f32[248,128]{1,0:T(8,128)S(1)} %get-tuple-element.50), channel_id=1, source_target_pairs={{0,8},{4,12},{8,0},{12,4},{16,24},{20,28},{24,16},{28,20},{1,9},{5... | collective-permute-start | bytes 380936 | tf_op jit(solution)/shard_map/ppermute | solution.py:545
  50.0 5.8 %collective-permute-start.9 = (f32[248,128]{1,0:T(8,128)S(1)}, f32[248,128]{1,0:T(8,128)S(1)}, u32[]{:S(2)}, u32[]{:S(2)}) collective-permute-start(f32[248,128]{1,0:T(8,128)S(1)} %get-tuple-element.51), channel_id=1, source_target_pairs={{0,12},{4,8},{8,4},{12,0},{16,28},{20,24},{24,20},{28,16},{1,13},{... | collective-permute-start | bytes 380936 | tf_op jit(solution)/shard_map/ppermute | solution.py:545
  57.1 7.1 %collective-permute-start.14 = (f32[128,128]{1,0:T(8,128)S(1)}, f32[128,128]{1,0:T(8,128)S(1)}, u32[]{:S(2)}, u32[]{:S(2)}) collective-permute-start(f32[128,128]{1,0:T(8,128)S(1)} %get-tuple-element.57), channel_id=1, source_target_pairs={{0,8},{1,9},{2,10},{3,11},{4,12},{5,13},{6,14},{7,15},{8,16},{9,17... | collective-permute-start | bytes 196616 | tf_op jit(solution)/shard_map/ppermute | solution.py:623
  59.3 6.3 %collective-permute-start.15 = (f32[128,128]{1,0:T(8,128)S(1)}, f32[128,128]{1,0:T(8,128)S(1)}, u32[]{:S(2)}, u32[]{:S(2)}) collective-permute-start(f32[128,128]{1,0:T(8,128)S(1)} %get-tuple-element.57), channel_id=1, source_target_pairs={{0,16},{1,17},{2,18},{3,19},{4,20},{5,21},{6,22},{7,23},{8,24},{9,... | collective-permute-start | bytes 196616 | tf_op jit(solution)/shard_map/ppermute | solution.py:623
  61.4 4.9 %collective-permute-start.16 = (f32[128,128]{1,0:T(8,128)S(1)}, f32[128,128]{1,0:T(8,128)S(1)}, u32[]{:S(2)}, u32[]{:S(2)}) collective-permute-start(f32[128,128]{1,0:T(8,128)S(1)} %get-tuple-element.57), channel_id=1, source_target_pairs={{0,24},{1,25},{2,26},{3,27},{4,28},{5,29},{6,30},{7,31},{8,0},{9,1... | collective-permute-start | bytes 196616 | tf_op jit(solution)/shard_map/ppermute | solution.py:623
  66.3 6.6 %collective-permute-start.17 = (f32[128,128]{1,0:T(8,128)S(1)}, f32[128,128]{1,0:T(8,128)S(1)}, u32[]{:S(2)}, u32[]{:S(2)}) collective-permute-start(f32[128,128]{1,0:T(8,128)S(1)} %get-tuple-element.63), channel_id=1, source_target_pairs={{0,8},{1,9},{2,10},{3,11},{4,12},{5,13},{6,14},{7,15},{8,16},{9,17... | collective-permute-start | bytes 196616 | tf_op jit(solution)/shard_map/ppermute | solution.py:623
  67.5 6.8 %collective-permute-start.18 = (f32[128,128]{1,0:T(8,128)S(1)}, f32[128,128]{1,0:T(8,128)S(1)}, u32[]{:S(2)}, u32[]{:S(2)}) collective-permute-start(f32[128,128]{1,0:T(8,128)S(1)} %get-tuple-element.63), channel_id=1, source_target_pairs={{0,16},{1,17},{2,18},{3,19},{4,20},{5,21},{6,22},{7,23},{8,24},{9,... | collective-permute-start | bytes 196616 | tf_op jit(solution)/shard_map/ppermute | solution.py:623
  71.2 4.3 %collective-permute-start.19 = (f32[128,128]{1,0:T(8,128)S(1)}, f32[128,128]{1,0:T(8,128)S(1)}, u32[]{:S(2)}, u32[]{:S(2)}) collective-permute-start(f32[128,128]{1,0:T(8,128)S(1)} %get-tuple-element.63), channel_id=1, source_target_pairs={{0,24},{1,25},{2,26},{3,27},{4,28},{5,29},{6,30},{7,31},{8,0},{9,1... | collective-permute-start | bytes 196616 | tf_op jit(solution)/shard_map/ppermute | solution.py:623
  75.6 9.3 %collective-permute-start.20 = (f32[1024,128]{1,0:T(8,128)S(1)}, f32[1024,128]{1,0:T(8,128)S(1)}, u32[]{:S(2)}, u32[]{:S(2)}) collective-permute-start(f32[1024,128]{1,0:T(8,128)S(1)} %constant_dynamic-update-slice_fusion), channel_id=1, source_target_pairs={{0,1},{1,0},{2,3},{3,2},{4,5},{5,4},{6,7},{7,6},{8,9},{9,8},{10,11... | collective-permute-start | bytes 1572872 | tf_op jit(solution)/shard_map/ppermute | solution.py:638
  75.7 9.2 %collective-permute-start.25 = (f32[512,128]{1,0:T(8,128)S(1)}, f32[512,128]{1,0:T(8,128)S(1)}, u32[]{:S(2)}, u32[]{:S(2)}) collective-permute-start(f32[512,128]{1,0:T(8,128)S(1)} %pad_maximum_fusion.refs_0_), channel_id=1, source_target_pairs={{0,2},{1,3},{2,0},{3,1},{4,6},{5,7},{6,4},{7,5},{8,10},{9,11},{10,... | collective-permute-start | bytes 786440 | tf_op jit(solution)/shard_map/ppermute | solution.py:630
  77.2 13.5 %collective-permute-start.21 = (f32[512,128]{1,0:T(8,128)S(1)}, f32[512,128]{1,0:T(8,128)S(1)}, u32[]{:S(2)}, u32[]{:S(2)}) collective-permute-start(f32[512,128]{1,0:T(8,128)S(1)} %pad_maximum_fusion.refs_0_), channel_id=1, source_target_pairs={{0,6},{1,7},{2,4},{3,5},{4,2},{5,3},{6,0},{7,1},{8,14},{9,15},{10,... | collective-permute-start | bytes 786440 | tf_op jit(solution)/shard_map/ppermute | solution.py:630
  78.4 13.7 %collective-permute-start.26 = (f32[512,128]{1,0:T(8,128)S(1)}, f32[512,128]{1,0:T(8,128)S(1)}, u32[]{:S(2)}, u32[]{:S(2)}) collective-permute-start(f32[512,128]{1,0:T(8,128)S(1)} %pad_maximum_fusion.refs_0_), channel_id=1, source_target_pairs={{0,4},{1,5},{2,6},{3,7},{4,0},{5,1},{6,2},{7,3},{8,12},{9,13},{10,... | collective-permute-start | bytes 786440 | tf_op jit(solution)/shard_map/ppermute | solution.py:630
  79.2 13.4 %collective-permute-start.27 = (f32[512,128]{1,0:T(8,128)S(1)}, f32[512,128]{1,0:T(8,128)S(1)}, u32[]{:S(2)}, u32[]{:S(2)}) collective-permute-start(f32[512,128]{1,0:T(8,128)S(1)} %pad_maximum_fusion.refs_0_), channel_id=1, source_target_pairs={{0,1},{1,0},{2,3},{3,2},{4,5},{5,4},{6,7},{7,6},{8,9},{9,8},{10,11... | collective-permute-start | bytes 786440 | tf_op jit(solution)/shard_map/ppermute | solution.py:636
  84.9 8.7 %collective-permute-start.28 = (f32[512,128]{1,0:T(8,128)S(1)}, f32[512,128]{1,0:T(8,128)S(1)}, u32[]{:S(2)}, u32[]{:S(2)}) collective-permute-start(f32[512,128]{1,0:T(8,128)S(1)} %collective-permute-done.25.refs_1_), channel_id=1, source_target_pairs={{0,1},{1,0},{2,3},{3,2},{4,5},{5,4},{6,7},{7,6},{8,9},{9,8},{10,11... | collective-permute-start | bytes 786440 | tf_op jit(solution)/shard_map/ppermute | solution.py:644
  90.7 30.5 %collective-permute-start.22 = (f32[1536,128]{1,0:T(8,128)S(1)}, f32[1536,128]{1,0:T(8,128)S(1)}, u32[]{:S(2)}, u32[]{:S(2)}) collective-permute-start(f32[1536,128]{1,0:T(8,128)S(1)} %slice_dynamic-update-slice_fusion.2), channel_id=1, source_target_pairs={{0,2},{1,3},{2,0},{3,1},{4,6},{5,7},{6,4},{7,5},{8,10},{9,11},{10,... | collective-permute-start | bytes 2359304 | tf_op jit(solution)/shard_map/ppermute | solution.py:630
  92.1 3.4 %collective-permute-start.29 = (f32[512,128]{1,0:T(8,128)S(1)}, f32[512,128]{1,0:T(8,128)S(1)}, u32[]{:S(2)}, u32[]{:S(2)}) collective-permute-start(f32[512,128]{1,0:T(8,128)S(1)} %collective-permute-done.26.refs_2_), channel_id=1, source_target_pairs={{0,1},{1,0},{2,3},{3,2},{4,5},{5,4},{6,7},{7,6},{8,9},{9,8},{10,11... | collective-permute-start | bytes 786440 | tf_op jit(solution)/shard_map/ppermute | solution.py:644
  92.1 3.4 %collective-permute-start.30 = (f32[512,128]{1,0:T(8,128)S(1)}, f32[512,128]{1,0:T(8,128)S(1)}, u32[]{:S(2)}, u32[]{:S(2)}) collective-permute-start(f32[512,128]{1,0:T(8,128)S(1)} %collective-permute-done.21.refs_3_), channel_id=1, source_target_pairs={{0,1},{1,0},{2,3},{3,2},{4,5},{5,4},{6,7},{7,6},{8,9},{9,8},{10,11... | collective-permute-start | bytes 786440 | tf_op jit(solution)/shard_map/ppermute | solution.py:644
  92.6 28.2 %collective-permute-start.23 = (f32[1024,128]{1,0:T(8,128)S(1)}, f32[1024,128]{1,0:T(8,128)S(1)}, u32[]{:S(2)}, u32[]{:S(2)}) collective-permute-start(f32[1024,128]{1,0:T(8,128)S(1)} %get-tuple-element.69), channel_id=1, source_target_pairs={{0,4},{1,5},{2,6},{3,7},{4,0},{5,1},{6,2},{7,3},{8,12},{9,13},{10,... | collective-permute-start | bytes 1572872 | tf_op jit(solution)/shard_map/ppermute | solution.py:630
  93.5 27.6 %collective-permute-start.24 = (f32[1024,128]{1,0:T(8,128)S(1)}, f32[1024,128]{1,0:T(8,128)S(1)}, u32[]{:S(2)}, u32[]{:S(2)}) collective-permute-start(f32[1024,128]{1,0:T(8,128)S(1)} %get-tuple-element.69), channel_id=1, source_target_pairs={{0,6},{1,7},{2,4},{3,5},{4,2},{5,3},{6,0},{7,1},{8,14},{9,15},{10,... | collective-permute-start | bytes 1572872 | tf_op jit(solution)/shard_map/ppermute | solution.py:630
  (5 other events, 29.3 us)

commit v3 on v2

--- a/solution.py
+++ b/solution.py
@@ -294,7 +294,8 @@
     work[rows:, :] = jnp.zeros((STRIP, 2 * rows), jnp.float32)
     wide[...] = jnp.zeros_like(wide)
     upper[...] = jnp.zeros_like(upper)
-    square[...] = jnp.zeros_like(square)
+    for j in range(1, FRONT):
+        square[j, :, width : width + j * rows] = jnp.zeros((rows, j * rows), jnp.float32)
     row_id = lax.broadcasted_iota(jnp.int32, (rows, 1), 0)
     col_id = lax.broadcasted_iota(jnp.int32, (1, rows), 1)
     eye = (row_id == col_id).astype(jnp.float32)
@@ -449,8 +450,10 @@
     device = meta[2]
     stride = pts_count // BAND
     gather(gathered, sides, meta, clusters, ring)
-    wide[...] = jnp.zeros_like(wide)
     for j in range(FRONT):
+        if j:
+            clear = jnp.zeros((j * rows, rows), jnp.float32)
+            wide[0 : j * rows, j * rows : (j + 1) * rows] = clear
         for i in range(j, BEFORE):
             e = BEFORE + j - i
             home = lax.rem(start + j + clusters - e, clusters)

time: 125 us -> 125 us (level)
  no operation moved by 1% of the time
where the time goes in v3:
time: 125 us
  waiting for transfers between devices  46.8 us (37%)
  starting transfers between devices  39.7 us (32%)
  Pallas kernels  35.2 us (28%)
  local copies, waits for them, and re-layouts  1.58 us (1%)
  between operations  1.57 us (1%)
    pallas_call x5, Pallas kernels, call(): pl.pallas_call(kernel, out_shape=out_shapes, in_specs=[spec(s) for s in s...  35.2 us
    ppermute x14, waiting for transfers between devices, flip(): lax.ppermute(value, axis, [(p, p ^ bit + 1) for p in range(count)])  28.7 us
    ppermute x14, starting transfers between devices, flip(): lax.ppermute(value, axis, [(p, p ^ bit + 1) for p in range(count)])  19.4 us
    ppermute x6, starting transfers between devices, along(): moved.append(lax.ppermute(value, AXES, pairs))  12 us
    ppermute x6, waiting for transfers between devices, across(): moved.append(lax.ppermute(value, AXES, pairs))  11.8 us
    ppermute x6, starting transfers between devices, across(): moved.append(lax.ppermute(value, AXES, pairs))  7.75 us
    ppermute x6, waiting for transfers between devices, along(): moved.append(lax.ppermute(value, AXES, pairs))  6.3 us
  transfers between devices with their start and end apart: 31, of which 15 were waited for; matrix products, arithmetic and copies ran while one was open for 0% of the time, Pallas kernels for 20%

profile of v3, /device:TPU:0, one launch (start us, length us, event | category | flops | bytes accessed | tf_op | source)
XLA Modules:
  0.0 124.9 jit_solution(5385664997573264366)
XLA Ops:
  0.7 1.4 %copy.15 = bf16[1,6,128,3,256]{4,2,1,3,0:T(8,128)(2,1)S(1)} copy(bf16[1,6,128,3,256]{4,2,3,1,0:T(8,128)(2,1)} %param.8) | data formatting | bytes 2359296 | tf_op args[0]
  2.1 2.6 %shard_map.103 = (f32[352,128]{1,0:T(8,128)S(1)}, f32[352,128]{1,0:T(8,128)S(1)}, f32[352,128]{1,0:T(8,128)S(1)}, f32[352,128]{1,0:T(8,128)S(1)}, f32[352,128]{1...) custom-call(s32[8]{0:T(128)S(1)} %compare_select_fusion.1.meta, ...), custom_call_target="tpu_custom_call" | custom-call | flops 528482304 | bytes 2629632 | tf_op jit(solution)/shard_map/pallas_call | solution.py:44
  5.3 2.6 %collective-permute-start.1 = (f32[352,128]{1,0:T(8,128)S(1)}, f32[352,128]{1,0:T(8,128)S(1)}, u32[]{:S(2)}, u32[]{:S(2)}) collective-permute-start(f32[352,128]{1,0:T(8,128)S(1)} %get-tuple-element.42), channel_id=1, source_target_pairs={{0,2},{1,3},{2,0},{3,1},{4,6},{5,7},{6,4},{7,5},{8,10},{9,11},{10,... | collective-permute-start | bytes 540680 | tf_op jit(solution)/shard_map/ppermute | solution.py:548
  7.9 1.8 %collective-permute-start.3 = (f32[352,128]{1,0:T(8,128)S(1)}, f32[352,128]{1,0:T(8,128)S(1)}, u32[]{:S(2)}, u32[]{:S(2)}) collective-permute-start(f32[352,128]{1,0:T(8,128)S(1)} %get-tuple-element.44), channel_id=1, source_target_pairs={{0,4},{1,5},{2,6},{3,7},{4,0},{5,1},{6,2},{7,3},{8,12},{9,13},{10,... | collective-permute-start | bytes 540680 | tf_op jit(solution)/shard_map/ppermute | solution.py:548
  9.7 2.6 %collective-permute-start.5 = (f32[352,128]{1,0:T(8,128)S(1)}, f32[352,128]{1,0:T(8,128)S(1)}, u32[]{:S(2)}, u32[]{:S(2)}) collective-permute-start(f32[352,128]{1,0:T(8,128)S(1)} %get-tuple-element.46), channel_id=1, source_target_pairs={{0,6},{1,7},{2,4},{3,5},{4,2},{5,3},{6,0},{7,1},{8,14},{9,15},{10,... | collective-permute-start | bytes 540680 | tf_op jit(solution)/shard_map/ppermute | solution.py:548
  13.3 1.6 %collective-permute-start.6 = (f32[352,128]{1,0:T(8,128)S(1)}, f32[352,128]{1,0:T(8,128)S(1)}, u32[]{:S(2)}, u32[]{:S(2)}) collective-permute-start(f32[352,128]{1,0:T(8,128)S(1)} %get-tuple-element.47), channel_id=1, source_target_pairs={{0,7},{1,6},{2,5},{3,4},{4,3},{5,2},{6,1},{7,0},{8,15},{9,14},{10,... | collective-permute-start | bytes 540680 | tf_op jit(solution)/shard_map/ppermute | solution.py:548
  14.9 1.8 %collective-permute-done.2.refs_3_ = f32[352,128]{1,0:T(8,128)S(1)} collective-permute-done((f32[352,128]{1,0:T(8,128)S(1)}, f32[352,128]{1,0:T(8,128)S(1)}, u32[]{:S(2)}, u32[]{:S(2)}) %collective-permute-start.2) | collective-permute-done | bytes 180256 | tf_op jit(solution)/shard_map/ppermute | solution.py:548
  16.7 8.9 %collective-permute-done.4.refs_5_ = f32[352,128]{1,0:T(8,128)S(1)} collective-permute-done((f32[352,128]{1,0:T(8,128)S(1)}, f32[352,128]{1,0:T(8,128)S(1)}, u32[]{:S(2)}, u32[]{:S(2)}) %collective-permute-start.4) | collective-permute-done | bytes 180256 | tf_op jit(solution)/shard_map/ppermute | solution.py:548
  25.6 2.2 %shard_map.104 = (f32[248,128]{1,0:T(8,128)S(1)}, f32[248,128]{1,0:T(8,128)S(1)}, f32[248,128]{1,0:T(8,128)S(1)}, f32[248,128]{1,0:T(8,128)S(1)}, f32[248,128]{1...) custom-call(s32[8]{0:T(128)S(1)} %copy-done.1, ...), custom_call_target="tpu_custom_call" | custom-call | bytes 2457600 | tf_op jit(solution)/shard_map/pallas_call | solution.py:44
  27.8 3.0 %collective-permute-start.10 = (f32[248,128]{1,0:T(8,128)S(1)}, f32[248,128]{1,0:T(8,128)S(1)}, u32[]{:S(2)}, u32[]{:S(2)}) collective-permute-start(f32[248,128]{1,0:T(8,128)S(1)} %get-tuple-element.52), channel_id=1, source_target_pairs={{0,16},{4,20},{8,24},{12,28},{16,0},{20,4},{24,8},{28,12},{1,17},{... | collective-permute-start | bytes 380936 | tf_op jit(solution)/shard_map/ppermute | solution.py:548
  30.8 1.3 %collective-permute-start.11 = (f32[248,128]{1,0:T(8,128)S(1)}, f32[248,128]{1,0:T(8,128)S(1)}, u32[]{:S(2)}, u32[]{:S(2)}) collective-permute-start(f32[248,128]{1,0:T(8,128)S(1)} %get-tuple-element.53), channel_id=1, source_target_pairs={{0,20},{4,16},{8,28},{12,24},{16,4},{20,0},{24,12},{28,8},{1,21},{... | collective-permute-start | bytes 380936 | tf_op jit(solution)/shard_map/ppermute | solution.py:548
  32.1 3.6 %collective-permute-start.12 = (f32[248,128]{1,0:T(8,128)S(1)}, f32[248,128]{1,0:T(8,128)S(1)}, u32[]{:S(2)}, u32[]{:S(2)}) collective-permute-start(f32[248,128]{1,0:T(8,128)S(1)} %get-tuple-element.54), channel_id=1, source_target_pairs={{0,24},{4,28},{8,16},{12,20},{16,8},{20,12},{24,0},{28,4},{1,25},{... | collective-permute-start | bytes 380936 | tf_op jit(solution)/shard_map/ppermute | solution.py:548
  35.7 1.7 %collective-permute-start.7 = (f32[248,128]{1,0:T(8,128)S(1)}, f32[248,128]{1,0:T(8,128)S(1)}, u32[]{:S(2)}, u32[]{:S(2)}) collective-permute-start(f32[248,128]{1,0:T(8,128)S(1)} %get-tuple-element.49), channel_id=1, source_target_pairs={{0,4},{4,0},{8,12},{12,8},{16,20},{20,16},{24,28},{28,24},{1,5},{5... | collective-permute-start | bytes 380936 | tf_op jit(solution)/shard_map/ppermute | solution.py:548
  37.4 8.6 %collective-permute-done.10.refs_4_ = f32[248,128]{1,0:T(8,128)S(1)} collective-permute-done((f32[248,128]{1,0:T(8,128)S(1)}, f32[248,128]{1,0:T(8,128)S(1)}, u32[]{:S(2)}, u32[]{:S(2)}) %collective-permute-start.10) | collective-permute-done | bytes 127008 | tf_op jit(solution)/shard_map/ppermute | solution.py:548
  46.4 3.5 %collective-permute-done.11.refs_5_ = f32[248,128]{1,0:T(8,128)S(1)} collective-permute-done((f32[248,128]{1,0:T(8,128)S(1)}, f32[248,128]{1,0:T(8,128)S(1)}, u32[]{:S(2)}, u32[]{:S(2)}) %collective-permute-start.11) | collective-permute-done | bytes 127008 | tf_op jit(solution)/shard_map/ppermute | solution.py:548
  51.1 4.7 %collective-permute-done.9.refs_3_ = f32[248,128]{1,0:T(8,128)S(1)} collective-permute-done((f32[248,128]{1,0:T(8,128)S(1)}, f32[248,128]{1,0:T(8,128)S(1)}, u32[]{:S(2)}, u32[]{:S(2)}) %collective-permute-start.9) | collective-permute-done | bytes 127008 | tf_op jit(solution)/shard_map/ppermute | solution.py:548
  55.8 1.4 %shard_map.105 = (f32[256,128]{1,0:T(8,128)S(1)}, f32[256,128]{1,0:T(8,128)S(1)}, f32[256,128]{1,0:T(8,128)S(1)}, f32[256,128]{1,0:T(8,128)S(1)}, f32[128,128]{1...) custom-call(s32[8]{0:T(128)S(1)} %copy-done.1, s32[8]{0:T(128)S(1)} %compare_select_fusion.1.meta, ...), custom_call_target="tpu_custom_call" | custom-call | bytes 1703936 | tf_op jit(solution)/shard_map/pallas_call | solution.py:44
  57.1 2.1 %collective-permute-start.14 = (f32[128,128]{1,0:T(8,128)S(1)}, f32[128,128]{1,0:T(8,128)S(1)}, u32[]{:S(2)}, u32[]{:S(2)}) collective-permute-start(f32[128,128]{1,0:T(8,128)S(1)} %get-tuple-element.57), channel_id=1, source_target_pairs={{0,8},{1,9},{2,10},{3,11},{4,12},{5,13},{6,14},{7,15},{8,16},{9,17... | collective-permute-start | bytes 196616 | tf_op jit(solution)/shard_map/ppermute | solution.py:626
  59.3 2.1 %collective-permute-start.15 = (f32[128,128]{1,0:T(8,128)S(1)}, f32[128,128]{1,0:T(8,128)S(1)}, u32[]{:S(2)}, u32[]{:S(2)}) collective-permute-start(f32[128,128]{1,0:T(8,128)S(1)} %get-tuple-element.57), channel_id=1, source_target_pairs={{0,16},{1,17},{2,18},{3,19},{4,20},{5,21},{6,22},{7,23},{8,24},{9,... | collective-permute-start | bytes 196616 | tf_op jit(solution)/shard_map/ppermute | solution.py:626
  61.4 2.8 %collective-permute-start.16 = (f32[128,128]{1,0:T(8,128)S(1)}, f32[128,128]{1,0:T(8,128)S(1)}, u32[]{:S(2)}, u32[]{:S(2)}) collective-permute-start(f32[128,128]{1,0:T(8,128)S(1)} %get-tuple-element.57), channel_id=1, source_target_pairs={{0,24},{1,25},{2,26},{3,27},{4,28},{5,29},{6,30},{7,31},{8,0},{9,1... | collective-permute-start | bytes 196616 | tf_op jit(solution)/shard_map/ppermute | solution.py:626
  64.2 1.4 %collective-permute-done.15 = f32[128,128]{1,0:T(8,128)S(1)} collective-permute-done((f32[128,128]{1,0:T(8,128)S(1)}, f32[128,128]{1,0:T(8,128)S(1)}, u32[]{:S(2)}, u32[]{:S(2)}) %collective-permute-start.15) | collective-permute-done | bytes 65568 | tf_op jit(solution)/shard_map/ppermute | solution.py:626
  66.3 1.2 collective-permute-start.17
  67.5 3.7 %collective-permute-start.18 = (f32[128,128]{1,0:T(8,128)S(1)}, f32[128,128]{1,0:T(8,128)S(1)}, u32[]{:S(2)}, u32[]{:S(2)}) collective-permute-start(f32[128,128]{1,0:T(8,128)S(1)} %get-tuple-element.63), channel_id=1, source_target_pairs={{0,16},{1,17},{2,18},{3,19},{4,20},{5,21},{6,22},{7,23},{8,24},{9,... | collective-permute-start | bytes 196616 | tf_op jit(solution)/shard_map/ppermute | solution.py:626
  71.2 1.7 %collective-permute-done.17 = f32[128,128]{1,0:T(8,128)S(1)} collective-permute-done((f32[128,128]{1,0:T(8,128)S(1)}, f32[128,128]{1,0:T(8,128)S(1)}, u32[]{:S(2)}, u32[]{:S(2)}) %collective-permute-start.17) | collective-permute-done | bytes 65568 | tf_op jit(solution)/shard_map/ppermute | solution.py:626
  72.9 1.4 %collective-permute-done.18 = f32[128,128]{1,0:T(8,128)S(1)} collective-permute-done((f32[128,128]{1,0:T(8,128)S(1)}, f32[128,128]{1,0:T(8,128)S(1)}, u32[]{:S(2)}, u32[]{:S(2)}) %collective-permute-start.18) | collective-permute-done | bytes 65568 | tf_op jit(solution)/shard_map/ppermute | solution.py:626
  75.7 1.6 %collective-permute-start.25 = (f32[512,128]{1,0:T(8,128)S(1)}, f32[512,128]{1,0:T(8,128)S(1)}, u32[]{:S(2)}, u32[]{:S(2)}) collective-permute-start(f32[512,128]{1,0:T(8,128)S(1)} %pad_maximum_fusion.refs_0_), channel_id=1, source_target_pairs={{0,2},{1,3},{2,0},{3,1},{4,6},{5,7},{6,4},{7,5},{8,10},{9,11},{10,... | collective-permute-start | bytes 786440 | tf_op jit(solution)/shard_map/ppermute | solution.py:633
  79.2 5.7 %collective-permute-done.25.refs_1_ = f32[512,128]{1,0:T(8,128)S(1)} collective-permute-done((f32[512,128]{1,0:T(8,128)S(1)}, f32[512,128]{1,0:T(8,128)S(1)}, u32[]{:S(2)}, u32[]{:S(2)}) %collective-permute-start.25) | collective-permute-done | bytes 262176 | tf_op jit(solution)/shard_map/ppermute | solution.py:633
  85.0 5.7 %collective-permute-done.21.refs_3_ = f32[512,128]{1,0:T(8,128)S(1)} collective-permute-done((f32[512,128]{1,0:T(8,128)S(1)}, f32[512,128]{1,0:T(8,128)S(1)}, u32[]{:S(2)}, u32[]{:S(2)}) %collective-permute-start.21) | collective-permute-done | bytes 262176 | tf_op jit(solution)/shard_map/ppermute | solution.py:633
  90.7 1.4 %collective-permute-start.22 = (f32[1536,128]{1,0:T(8,128)S(1)}, f32[1536,128]{1,0:T(8,128)S(1)}, u32[]{:S(2)}, u32[]{:S(2)}) collective-permute-start(f32[1536,128]{1,0:T(8,128)S(1)} %slice_dynamic-update-slice_fusion.2), channel_id=1, source_target_pairs={{0,2},{1,3},{2,0},{3,1},{4,6},{5,7},{6,4},{7,5},{8,10},{9,11},{10,... | collective-permute-start | bytes 2359304 | tf_op jit(solution)/shard_map/ppermute | solution.py:633
  93.5 1.9 %collective-permute-start.24 = (f32[1024,128]{1,0:T(8,128)S(1)}, f32[1024,128]{1,0:T(8,128)S(1)}, u32[]{:S(2)}, u32[]{:S(2)}) collective-permute-start(f32[1024,128]{1,0:T(8,128)S(1)} %get-tuple-element.69), channel_id=1, source_target_pairs={{0,6},{1,7},{2,4},{3,5},{4,2},{5,3},{6,0},{7,1},{8,14},{9,15},{10,... | collective-permute-start | bytes 1572872 | tf_op jit(solution)/shard_map/ppermute | solution.py:633
  95.5 25.3 %shard_map.106 = (f32[1440,128]{1,0:T(8,128)S(1)}, bf16[512,512]{1,0:T(8,128)(2,1)S(1)}, bf16[512,512]{1,0:T(8,128)(2,1)S(1)}, bf16[904,512]{1,0:T(8,128)(2,1)S(1)}, bf16[904,512]{1,0:T(8,128)(2,1)S(1)}) custom-call(s32[8]{0:T(128)S(1)} %compare_select_fusion.1.meta, s32[1]{0:T(128)S(6)} %copy.29.front, s32[8]{0:T(128)S(1)} %copy-done.1, ...), custom_call_target="tpu_custom_call" | custom-call | flops 5033164800 | bytes 5750784 | tf_op jit(solution)/shard_map/pallas_call | solution.py:44
  121.2 3.7 %shard_map.107 = (f32[8,128,128]{2,1,0:T(8,128)}, f32[1,128]{1,0:T(1,128)}, f32[2304,128]{1,0:T(8,128)}) custom-call(s32[8]{0:T(128)S(1)} %compare_select_fusion.1.meta, s32[1]{0:T(128)S(6)} %copy.29.front, s32[8]{0:T(128)S(1)} %copy-done.1, f32[32,128]{1,0:T(8,128)S(1)} %get-tuple-element.56.reduced, f32[512,128]{1,0:T(8,128)S(1)} %pad_maximum_fusion.1.refs_0_, ...), custom_call_target="tpu_custom_call" | custom-call | flops 2516582400 | bytes 8110592 | tf_op jit(solution)/shard_map/pallas_call | solution.py:44
  (62 shorter events, 8.5 us)
Async XLA Ops:
  4.7 51.0 %copy-start = (f32[32,128]{1,0:T(8,128)S(1)}, f32[32,128]{1,0:T(8,128)}, u32[]{:S(2)}) copy-start(f32[32,128]{1,0:T(8,128)} %damping.1) | copy-start | bytes 49156
  4.8 4.9 %collective-permute-start = (f32[352,128]{1,0:T(8,128)S(1)}, f32[352,128]{1,0:T(8,128)S(1)}, u32[]{:S(2)}, u32[]{:S(2)}) collective-permute-start(f32[352,128]{1,0:T(8,128)S(1)} %get-tuple-element.41), channel_id=1, source_target_pairs={{0,1},{1,0},{2,3},{3,2},{4,5},{5,4},{6,7},{7,6},{8,9},{9,8},{10,11... | collective-permute-start | bytes 540680 | tf_op jit(solution)/shard_map/ppermute | solution.py:548
  5.3 8.0 %collective-permute-start.1 = (f32[352,128]{1,0:T(8,128)S(1)}, f32[352,128]{1,0:T(8,128)S(1)}, u32[]{:S(2)}, u32[]{:S(2)}) collective-permute-start(f32[352,128]{1,0:T(8,128)S(1)} %get-tuple-element.42), channel_id=1, source_target_pairs={{0,2},{1,3},{2,0},{3,1},{4,6},{5,7},{6,4},{7,5},{8,10},{9,11},{10,... | collective-permute-start | bytes 540680 | tf_op jit(solution)/shard_map/ppermute | solution.py:548
  7.9 8.8 %collective-permute-start.2 = (f32[352,128]{1,0:T(8,128)S(1)}, f32[352,128]{1,0:T(8,128)S(1)}, u32[]{:S(2)}, u32[]{:S(2)}) collective-permute-start(f32[352,128]{1,0:T(8,128)S(1)} %get-tuple-element.43), channel_id=1, source_target_pairs={{0,3},{1,2},{2,1},{3,0},{4,7},{5,6},{6,5},{7,4},{8,11},{9,10},{10,... | collective-permute-start | bytes 540680 | tf_op jit(solution)/shard_map/ppermute | solution.py:548
  7.9 8.8 %collective-permute-start.3 = (f32[352,128]{1,0:T(8,128)S(1)}, f32[352,128]{1,0:T(8,128)S(1)}, u32[]{:S(2)}, u32[]{:S(2)}) collective-permute-start(f32[352,128]{1,0:T(8,128)S(1)} %get-tuple-element.44), channel_id=1, source_target_pairs={{0,4},{1,5},{2,6},{3,7},{4,0},{5,1},{6,2},{7,3},{8,12},{9,13},{10,... | collective-permute-start | bytes 540680 | tf_op jit(solution)/shard_map/ppermute | solution.py:548
  9.7 15.9 %collective-permute-start.4 = (f32[352,128]{1,0:T(8,128)S(1)}, f32[352,128]{1,0:T(8,128)S(1)}, u32[]{:S(2)}, u32[]{:S(2)}) collective-permute-start(f32[352,128]{1,0:T(8,128)S(1)} %get-tuple-element.45), channel_id=1, source_target_pairs={{0,5},{1,4},{2,7},{3,6},{4,1},{5,0},{6,3},{7,2},{8,13},{9,12},{10,... | collective-permute-start | bytes 540680 | tf_op jit(solution)/shard_map/ppermute | solution.py:548
  9.7 15.9 %collective-permute-start.5 = (f32[352,128]{1,0:T(8,128)S(1)}, f32[352,128]{1,0:T(8,128)S(1)}, u32[]{:S(2)}, u32[]{:S(2)}) collective-permute-start(f32[352,128]{1,0:T(8,128)S(1)} %get-tuple-element.46), channel_id=1, source_target_pairs={{0,6},{1,7},{2,4},{3,5},{4,2},{5,3},{6,0},{7,1},{8,14},{9,15},{10,... | collective-permute-start | bytes 540680 | tf_op jit(solution)/shard_map/ppermute | solution.py:548
  13.3 12.3 %collective-permute-start.6 = (f32[352,128]{1,0:T(8,128)S(1)}, f32[352,128]{1,0:T(8,128)S(1)}, u32[]{:S(2)}, u32[]{:S(2)}) collective-permute-start(f32[352,128]{1,0:T(8,128)S(1)} %get-tuple-element.47), channel_id=1, source_target_pairs={{0,7},{1,6},{2,5},{3,4},{4,3},{5,2},{6,1},{7,0},{8,15},{9,14},{10,... | collective-permute-start | bytes 540680 | tf_op jit(solution)/shard_map/ppermute | solution.py:548
  27.8 18.1 %collective-permute-start.10 = (f32[248,128]{1,0:T(8,128)S(1)}, f32[248,128]{1,0:T(8,128)S(1)}, u32[]{:S(2)}, u32[]{:S(2)}) collective-permute-start(f32[248,128]{1,0:T(8,128)S(1)} %get-tuple-element.52), channel_id=1, source_target_pairs={{0,16},{4,20},{8,24},{12,28},{16,0},{20,4},{24,8},{28,12},{1,17},{... | collective-permute-start | bytes 380936 | tf_op jit(solution)/shard_map/ppermute | solution.py:548
  30.8 19.2 %collective-permute-start.11 = (f32[248,128]{1,0:T(8,128)S(1)}, f32[248,128]{1,0:T(8,128)S(1)}, u32[]{:S(2)}, u32[]{:S(2)}) collective-permute-start(f32[248,128]{1,0:T(8,128)S(1)} %get-tuple-element.53), channel_id=1, source_target_pairs={{0,20},{4,16},{8,28},{12,24},{16,4},{20,0},{24,12},{28,8},{1,21},{... | collective-permute-start | bytes 380936 | tf_op jit(solution)/shard_map/ppermute | solution.py:548
  32.1 18.7 %collective-permute-start.12 = (f32[248,128]{1,0:T(8,128)S(1)}, f32[248,128]{1,0:T(8,128)S(1)}, u32[]{:S(2)}, u32[]{:S(2)}) collective-permute-start(f32[248,128]{1,0:T(8,128)S(1)} %get-tuple-element.54), channel_id=1, source_target_pairs={{0,24},{4,28},{8,16},{12,20},{16,8},{20,12},{24,0},{28,4},{1,25},{... | collective-permute-start | bytes 380936 | tf_op jit(solution)/shard_map/ppermute | solution.py:548
  35.7 15.1 %collective-permute-start.13 = (f32[248,128]{1,0:T(8,128)S(1)}, f32[248,128]{1,0:T(8,128)S(1)}, u32[]{:S(2)}, u32[]{:S(2)}) collective-permute-start(f32[248,128]{1,0:T(8,128)S(1)} %get-tuple-element.55), channel_id=1, source_target_pairs={{0,28},{4,24},{8,20},{12,16},{16,12},{20,8},{24,4},{28,0},{1,29},{... | collective-permute-start | bytes 380936 | tf_op jit(solution)/shard_map/ppermute | solution.py:548
  35.7 15.1 %collective-permute-start.7 = (f32[248,128]{1,0:T(8,128)S(1)}, f32[248,128]{1,0:T(8,128)S(1)}, u32[]{:S(2)}, u32[]{:S(2)}) collective-permute-start(f32[248,128]{1,0:T(8,128)S(1)} %get-tuple-element.49), channel_id=1, source_target_pairs={{0,4},{4,0},{8,12},{12,8},{16,20},{20,16},{24,28},{28,24},{1,5},{5... | collective-permute-start | bytes 380936 | tf_op jit(solution)/shard_map/ppermute | solution.py:548
  45.9 5.2 %collective-permute-start.8 = (f32[248,128]{1,0:T(8,128)S(1)}, f32[248,128]{1,0:T(8,128)S(1)}, u32[]{:S(2)}, u32[]{:S(2)}) collective-permute-start(f32[248,128]{1,0:T(8,128)S(1)} %get-tuple-element.50), channel_id=1, source_target_pairs={{0,8},{4,12},{8,0},{12,4},{16,24},{20,28},{24,16},{28,20},{1,9},{5... | collective-permute-start | bytes 380936 | tf_op jit(solution)/shard_map/ppermute | solution.py:548
  50.0 5.8 %collective-permute-start.9 = (f32[248,128]{1,0:T(8,128)S(1)}, f32[248,128]{1,0:T(8,128)S(1)}, u32[]{:S(2)}, u32[]{:S(2)}) collective-permute-start(f32[248,128]{1,0:T(8,128)S(1)} %get-tuple-element.51), channel_id=1, source_target_pairs={{0,12},{4,8},{8,4},{12,0},{16,28},{20,24},{24,20},{28,16},{1,13},{... | collective-permute-start | bytes 380936 | tf_op jit(solution)/shard_map/ppermute | solution.py:548
  57.1 7.1 %collective-permute-start.14 = (f32[128,128]{1,0:T(8,128)S(1)}, f32[128,128]{1,0:T(8,128)S(1)}, u32[]{:S(2)}, u32[]{:S(2)}) collective-permute-start(f32[128,128]{1,0:T(8,128)S(1)} %get-tuple-element.57), channel_id=1, source_target_pairs={{0,8},{1,9},{2,10},{3,11},{4,12},{5,13},{6,14},{7,15},{8,16},{9,17... | collective-permute-start | bytes 196616 | tf_op jit(solution)/shard_map/ppermute | solution.py:626
  59.3 6.3 %collective-permute-start.15 = (f32[128,128]{1,0:T(8,128)S(1)}, f32[128,128]{1,0:T(8,128)S(1)}, u32[]{:S(2)}, u32[]{:S(2)}) collective-permute-start(f32[128,128]{1,0:T(8,128)S(1)} %get-tuple-element.57), channel_id=1, source_target_pairs={{0,16},{1,17},{2,18},{3,19},{4,20},{5,21},{6,22},{7,23},{8,24},{9,... | collective-permute-start | bytes 196616 | tf_op jit(solution)/shard_map/ppermute | solution.py:626
  61.4 4.9 %collective-permute-start.16 = (f32[128,128]{1,0:T(8,128)S(1)}, f32[128,128]{1,0:T(8,128)S(1)}, u32[]{:S(2)}, u32[]{:S(2)}) collective-permute-start(f32[128,128]{1,0:T(8,128)S(1)} %get-tuple-element.57), channel_id=1, source_target_pairs={{0,24},{1,25},{2,26},{3,27},{4,28},{5,29},{6,30},{7,31},{8,0},{9,1... | collective-permute-start | bytes 196616 | tf_op jit(solution)/shard_map/ppermute | solution.py:626
  66.3 6.6 %collective-permute-start.17 = (f32[128,128]{1,0:T(8,128)S(1)}, f32[128,128]{1,0:T(8,128)S(1)}, u32[]{:S(2)}, u32[]{:S(2)}) collective-permute-start(f32[128,128]{1,0:T(8,128)S(1)} %get-tuple-element.63), channel_id=1, source_target_pairs={{0,8},{1,9},{2,10},{3,11},{4,12},{5,13},{6,14},{7,15},{8,16},{9,17... | collective-permute-start | bytes 196616 | tf_op jit(solution)/shard_map/ppermute | solution.py:626
  67.5 6.8 %collective-permute-start.18 = (f32[128,128]{1,0:T(8,128)S(1)}, f32[128,128]{1,0:T(8,128)S(1)}, u32[]{:S(2)}, u32[]{:S(2)}) collective-permute-start(f32[128,128]{1,0:T(8,128)S(1)} %get-tuple-element.63), channel_id=1, source_target_pairs={{0,16},{1,17},{2,18},{3,19},{4,20},{5,21},{6,22},{7,23},{8,24},{9,... | collective-permute-start | bytes 196616 | tf_op jit(solution)/shard_map/ppermute | solution.py:626
  71.2 4.3 %collective-permute-start.19 = (f32[128,128]{1,0:T(8,128)S(1)}, f32[128,128]{1,0:T(8,128)S(1)}, u32[]{:S(2)}, u32[]{:S(2)}) collective-permute-start(f32[128,128]{1,0:T(8,128)S(1)} %get-tuple-element.63), channel_id=1, source_target_pairs={{0,24},{1,25},{2,26},{3,27},{4,28},{5,29},{6,30},{7,31},{8,0},{9,1... | collective-permute-start | bytes 196616 | tf_op jit(solution)/shard_map/ppermute | solution.py:626
  75.6 9.3 %collective-permute-start.20 = (f32[1024,128]{1,0:T(8,128)S(1)}, f32[1024,128]{1,0:T(8,128)S(1)}, u32[]{:S(2)}, u32[]{:S(2)}) collective-permute-start(f32[1024,128]{1,0:T(8,128)S(1)} %constant_dynamic-update-slice_fusion), channel_id=1, source_target_pairs={{0,1},{1,0},{2,3},{3,2},{4,5},{5,4},{6,7},{7,6},{8,9},{9,8},{10,11... | collective-permute-start | bytes 1572872 | tf_op jit(solution)/shard_map/ppermute | solution.py:641
  75.7 9.2 %collective-permute-start.25 = (f32[512,128]{1,0:T(8,128)S(1)}, f32[512,128]{1,0:T(8,128)S(1)}, u32[]{:S(2)}, u32[]{:S(2)}) collective-permute-start(f32[512,128]{1,0:T(8,128)S(1)} %pad_maximum_fusion.refs_0_), channel_id=1, source_target_pairs={{0,2},{1,3},{2,0},{3,1},{4,6},{5,7},{6,4},{7,5},{8,10},{9,11},{10,... | collective-permute-start | bytes 786440 | tf_op jit(solution)/shard_map/ppermute | solution.py:633
  77.2 13.5 %collective-permute-start.21 = (f32[512,128]{1,0:T(8,128)S(1)}, f32[512,128]{1,0:T(8,128)S(1)}, u32[]{:S(2)}, u32[]{:S(2)}) collective-permute-start(f32[512,128]{1,0:T(8,128)S(1)} %pad_maximum_fusion.refs_0_), channel_id=1, source_target_pairs={{0,6},{1,7},{2,4},{3,5},{4,2},{5,3},{6,0},{7,1},{8,14},{9,15},{10,... | collective-permute-start | bytes 786440 | tf_op jit(solution)/shard_map/ppermute | solution.py:633
  78.4 13.7 %collective-permute-start.26 = (f32[512,128]{1,0:T(8,128)S(1)}, f32[512,128]{1,0:T(8,128)S(1)}, u32[]{:S(2)}, u32[]{:S(2)}) collective-permute-start(f32[512,128]{1,0:T(8,128)S(1)} %pad_maximum_fusion.refs_0_), channel_id=1, source_target_pairs={{0,4},{1,5},{2,6},{3,7},{4,0},{5,1},{6,2},{7,3},{8,12},{9,13},{10,... | collective-permute-start | bytes 786440 | tf_op jit(solution)/shard_map/ppermute | solution.py:633
  79.2 13.4 %collective-permute-start.27 = (f32[512,128]{1,0:T(8,128)S(1)}, f32[512,128]{1,0:T(8,128)S(1)}, u32[]{:S(2)}, u32[]{:S(2)}) collective-permute-start(f32[512,128]{1,0:T(8,128)S(1)} %pad_maximum_fusion.refs_0_), channel_id=1, source_target_pairs={{0,1},{1,0},{2,3},{3,2},{4,5},{5,4},{6,7},{7,6},{8,9},{9,8},{10,11... | collective-permute-start | bytes 786440 | tf_op jit(solution)/shard_map/ppermute | solution.py:639
  84.9 8.7 %collective-permute-start.28 = (f32[512,128]{1,0:T(8,128)S(1)}, f32[512,128]{1,0:T(8,128)S(1)}, u32[]{:S(2)}, u32[]{:S(2)}) collective-permute-start(f32[512,128]{1,0:T(8,128)S(1)} %collective-permute-done.25.refs_1_), channel_id=1, source_target_pairs={{0,1},{1,0},{2,3},{3,2},{4,5},{5,4},{6,7},{7,6},{8,9},{9,8},{10,11... | collective-permute-start | bytes 786440 | tf_op jit(solution)/shard_map/ppermute | solution.py:647
  90.7 30.5 %collective-permute-start.22 = (f32[1536,128]{1,0:T(8,128)S(1)}, f32[1536,128]{1,0:T(8,128)S(1)}, u32[]{:S(2)}, u32[]{:S(2)}) collective-permute-start(f32[1536,128]{1,0:T(8,128)S(1)} %slice_dynamic-update-slice_fusion.2), channel_id=1, source_target_pairs={{0,2},{1,3},{2,0},{3,1},{4,6},{5,7},{6,4},{7,5},{8,10},{9,11},{10,... | collective-permute-start | bytes 2359304 | tf_op jit(solution)/shard_map/ppermute | solution.py:633
  92.1 3.4 %collective-permute-start.29 = (f32[512,128]{1,0:T(8,128)S(1)}, f32[512,128]{1,0:T(8,128)S(1)}, u32[]{:S(2)}, u32[]{:S(2)}) collective-permute-start(f32[512,128]{1,0:T(8,128)S(1)} %collective-permute-done.26.refs_2_), channel_id=1, source_target_pairs={{0,1},{1,0},{2,3},{3,2},{4,5},{5,4},{6,7},{7,6},{8,9},{9,8},{10,11... | collective-permute-start | bytes 786440 | tf_op jit(solution)/shard_map/ppermute | solution.py:647
  92.1 3.4 %collective-permute-start.30 = (f32[512,128]{1,0:T(8,128)S(1)}, f32[512,128]{1,0:T(8,128)S(1)}, u32[]{:S(2)}, u32[]{:S(2)}) collective-permute-start(f32[512,128]{1,0:T(8,128)S(1)} %collective-permute-done.21.refs_3_), channel_id=1, source_target_pairs={{0,1},{1,0},{2,3},{3,2},{4,5},{5,4},{6,7},{7,6},{8,9},{9,8},{10,11... | collective-permute-start | bytes 786440 | tf_op jit(solution)/shard_map/ppermute | solution.py:647
  92.6 28.2 %collective-permute-start.23 = (f32[1024,128]{1,0:T(8,128)S(1)}, f32[1024,128]{1,0:T(8,128)S(1)}, u32[]{:S(2)}, u32[]{:S(2)}) collective-permute-start(f32[1024,128]{1,0:T(8,128)S(1)} %get-tuple-element.69), channel_id=1, source_target_pairs={{0,4},{1,5},{2,6},{3,7},{4,0},{5,1},{6,2},{7,3},{8,12},{9,13},{10,... | collective-permute-start | bytes 1572872 | tf_op jit(solution)/shard_map/ppermute | solution.py:633
  93.5 27.6 %collective-permute-start.24 = (f32[1024,128]{1,0:T(8,128)S(1)}, f32[1024,128]{1,0:T(8,128)S(1)}, u32[]{:S(2)}, u32[]{:S(2)}) collective-permute-start(f32[1024,128]{1,0:T(8,128)S(1)} %get-tuple-element.69), channel_id=1, source_target_pairs={{0,6},{1,7},{2,4},{3,5},{4,2},{5,3},{6,0},{7,1},{8,14},{9,15},{10,... | collective-permute-start | bytes 1572872 | tf_op jit(solution)/shard_map/ppermute | solution.py:633
  (5 other events, 29.3 us)
